TPU v7x, 32 devices: a whole 2x2x4 slice. The times are simulated.
32 devices in a mesh: segment: 2 (over x), dp: 16 (over z, y, core).
Axes of the slice: x: 2, y: 2, z: 4, core: 2. Of those that a mesh axis runs over, the one named last changes fastest.
Arguments:
- fine_inflow: bfloat16 [2, 16, 16, 16, 256], P('segment', 'dp'), may hold values from -250 to 250
- coarse_inflow: bfloat16 [2, 16, 8, 8, 512], P('segment', 'dp'), may hold values from -250 to 250
- fine_entries: bfloat16 [3, 16, 16, 16, 256], P(None, 'dp'), may hold values from -250 to 250
- fine_pending: bfloat16 [2, 2, 16, 16, 16, 256], P('segment', None, 'dp'), may hold values from -250 to 250, as said below
- coarse_pending: bfloat16 [2, 1, 16, 8, 8, 512], P('segment', None, 'dp'), may hold values from -250 to 250, as said below
- fine_kernels: bfloat16 [2, 2, 3, 3, 256, 256], P('segment'), may hold values from -0.125 to 0.125
- fine_mixing: bfloat16 [2, 256, 256], P('segment'), may hold values from -0.375 to 0.375
- fine_gains: float32 [2, 2, 256], P('segment'), may hold values from 0.5 to 1.5
- fine_shifts: float32 [2, 2, 256], P('segment'), may hold values from -3 to 3
- coarse_kernel: bfloat16 [2, 3, 3, 512, 512], P('segment'), may hold values from -0.09375 to 0.09375
- coarse_mixing: bfloat16 [2, 512, 512], P('segment'), may hold values from -0.25 to 0.25
- coarse_gains: float32 [2, 512], P('segment'), may hold values from 0.5 to 1.5
- coarse_shifts: float32 [2, 512], P('segment'), may hold values from -3 to 3
- descent_kernel: bfloat16 [2, 2, 256, 512], replicated, may hold values from -0.1875 to 0.1875
- upsample_kernel: bfloat16 [512, 2, 2, 256], replicated, may hold values from -0.25 to 0.25
Outputs:
- fine_stash: bfloat16 [2, 4, 16, 16, 16, 256], P('segment', None, 'dp')
- coarse_stash: bfloat16 [2, 4, 16, 8, 8, 512], P('segment', None, 'dp')
- fine_backlog: bfloat16 [2, 2, 16, 16, 16, 256], P('segment', None, 'dp')
- coarse_backlog: bfloat16 [2, 1, 16, 8, 8, 512], P('segment', None, 'dp')
Inputs may be any that keep to these rules, and one draw needn't show every extreme that they name: `fine_pending`: at segments 1 and above only the first 1 slots are read. `coarse_pending`: at segments below 1 only the first 0 slots are read.
All inputs are finite; a program needn't handle non-finite values.
Results may differ from a plain program's by a relative error of at most 0.017.
Values may be sent and summed in bfloat16 or wider, within the bound.
A program may use at most 64 MiB of HBM per device.

v0:
```python
import functools

import jax
import jax.numpy as jnp
from jax import lax
from jax.experimental import pallas as pl
from jax.experimental.pallas import tpu as pltpu
from jax.sharding import PartitionSpec as P

EPSILON = 1e-05
LANES = 128
MESH = pl.DeviceIdType.MESH
F32 = jnp.float32
BF16 = jnp.bfloat16


def dot(a, b):
    return jnp.dot(a, b, preferred_element_type=F32)


def side_shifts(x, side):
    cells = x.shape[0]
    column = lax.rem(lax.broadcasted_iota(jnp.int32, x.shape, 0), side)
    before = jnp.where(column == 0, 0.0, pltpu.roll(x, 1, 0))
    after = jnp.where(column == side - 1, 0.0, pltpu.roll(x, cells - 1, 0))
    return before, x, after


def spread_taps(x, cols, side):
    cells, width = x.shape
    edge = jnp.zeros((side, width), F32)
    for dc, part in enumerate(side_shifts(x, side)):
        above = jnp.concatenate([edge, part[: cells - side]], axis=0)
        below = jnp.concatenate([part[side:], edge], axis=0)
        for dr, moved in enumerate((above, part, below)):
            start = (3 * dr + dc) * width
            cols[:, start : start + width] = moved.astype(BF16)


def put_stats(h, out):
    width = h.shape[1]
    rows = width // LANES
    total = jnp.sum(h, axis=0, keepdims=True)
    square = jnp.sum(h * h, axis=0, keepdims=True)
    for row in range(rows):
        lanes = slice(row * LANES, (row + 1) * LANES)
        out[row : row + 1, :] = total[:, lanes]
        out[rows + row : rows + row + 1, :] = square[:, lanes]


def norm_terms(total, gain, shift, count):
    rows = total.shape[0] // 2
    sums = jnp.concatenate([total[row : row + 1] for row in range(rows)], axis=1)
    squares = jnp.concatenate([total[rows + row : rows + row + 1] for row in range(rows)], axis=1)
    center = sums * (1.0 / count)
    spread = jnp.maximum(squares * (1.0 / count) - center * center, 0.0)
    scale = lax.rsqrt(spread + EPSILON) * gain
    return scale, shift - center * scale


def kernel(
    dims,
    fine_in, coarse_in, entries, fine_pend, coarse_pend,
    wf_hbm, mixf_hbm, fgain, fshift, wc_hbm, mixc_hbm, cgain, cshift, wd_hbm, wu_hbm,
    fst_out, cst_out, fback_out, cback_out,
    wf, mixf, wc, mixc, wd, wu,
    fin, cin, upin, skf, skc, fst, cst, dbuf,
    xs, hf, hg, hc, upscr, colf, colc, zf, zc,
    statf, statc, gotf, gotc,
    wu4, wuf, load_sem, save_sem,
    fin_r, cin_r, up_r, skf_r, skc_r,
    fin_s, cin_s, up_s, skf_s, skc_s,
    gotf_r, gotc_r, statf_s, statc_s,
):
    nseg, ndp, ticks, fside, cside, hold_f, recv_f, hold_c, recv_c = dims
    half = nseg // 2
    seg = lax.axis_index("segment")
    me = lax.axis_index("dp")
    lower = seg < half
    upper = seg >= half
    turn = seg == half - 1
    after = lax.rem(seg + 1, nseg)
    mate = lax.rem(seg + half, nseg)

    def load(k, src, dst):
        return pltpu.make_async_copy(src, dst, load_sem.at[k])

    get_fine = load(0, fine_in, fin.at[0])
    get_wf0 = load(1, wf_hbm.at[0], wf.at[0])
    get_mixf = load(2, mixf_hbm, mixf)
    get_coarse = load(3, coarse_in, cin.at[0])
    get_mixc = load(4, mixc_hbm, mixc)
    get_wc = load(5, wc_hbm, wc)
    get_wf1 = load(6, wf_hbm.at[1], wf.at[1])
    get_wd = load(7, wd_hbm, wd)
    get_wu = load(11, wu_hbm, wu4)
    own_entries = load(8, entries, fin.at[pl.ds(1, ticks - 1)])
    own_fine = hold_f if hold_f > ticks else 0
    own_coarse = hold_c if hold_c > ticks else 0

    def own_pend(k, src, dst, count):
        return load(k, src.at[pl.ds(0, count)], dst.at[pl.ds(0, count)])

    barrier = pltpu.get_barrier_semaphore()
    offsets = sorted({1 % nseg, nseg - 1, half})

    def greet(k, carry):
        pl.semaphore_signal(
            barrier, inc=1, device_id=(seg, lax.rem(me + k, ndp)), device_id_type=MESH
        )
        return carry

    lax.fori_loop(1, ndp, greet, 0)
    for offset in offsets:
        pl.semaphore_signal(
            barrier, inc=1, device_id=(lax.rem(seg + offset, nseg), me), device_id_type=MESH
        )
    @pl.when(upper)
    def _():
        if recv_f:
            own_pend(9, fine_pend, skf, recv_f).start()

    for item in (get_fine, get_wf0, get_mixf, get_coarse, get_mixc, get_wc, get_wf1):
        item.start()

    @pl.when(lower)
    def _():
        if recv_c:
            own_pend(10, coarse_pend, skc, recv_c).start()
        if own_fine:
            own_pend(9, fine_pend, skf, own_fine).start()

    @pl.when(upper)
    def _():
        if own_coarse:
            own_pend(10, coarse_pend, skc, own_coarse).start()

    @pl.when(seg == 0)
    def _():
        own_entries.start()

    @pl.when(turn)
    def _():
        get_wd.start()

    @pl.when(seg == half)
    def _():
        get_wu.start()

    zf[...] = jnp.zeros_like(zf)
    zc[...] = jnp.zeros_like(zc)
    pl.semaphore_wait(barrier, ndp - 1 + len(offsets))

    def push(src, dst, ssem, rsem, to):
        return pltpu.make_async_remote_copy(
            src_ref=src, dst_ref=dst, send_sem=ssem, recv_sem=rsem,
            device_id=(to, me), device_id_type=MESH,
        )

    def send_skf(j):
        return push(skf.at[j], skf.at[recv_f + j], skf_s.at[j], skf_r.at[j], mate)

    def send_pend_f(j):
        return push(fine_pend.at[j], skf.at[recv_f + j], skf_s.at[j], skf_r.at[j], mate)

    def send_pend_c(j):
        return push(coarse_pend.at[j], skc.at[recv_c + j], skc_s.at[j], skc_r.at[j], mate)

    def send_skc(j):
        return push(skc.at[j], skc.at[recv_c + j], skc_s.at[j], skc_r.at[j], mate)

    def send_up(t):
        return push(cst.at[t], upin.at[t], up_s.at[t], up_r.at[t], after)

    def send_co(t):
        return push(cst.at[t], cin.at[t + 1], cin_s.at[t], cin_r.at[t], after)

    def send_down(t):
        return push(dbuf.at[t], cin.at[t + 1], cin_s.at[t], cin_r.at[t], after)

    def send_fo(t):
        return push(fst.at[t], fin.at[t + 1], fin_s.at[t], fin_r.at[t], after)

    def exchange(src, dst, ssem, rsem):
        def one(k, carry):
            pltpu.make_async_remote_copy(
                src_ref=src, dst_ref=dst.at[k - 1], send_sem=ssem, recv_sem=rsem,
                device_id=(seg, lax.rem(me + k, ndp)), device_id_type=MESH,
            ).start()
            return carry

        lax.fori_loop(1, ndp, one, 0)

    def whole(dst, ssem, rsem):
        return pltpu.make_async_remote_copy(
            src_ref=dst, dst_ref=dst, send_sem=ssem, recv_sem=rsem,
            device_id=(seg, lax.rem(me + 1, ndp)), device_id_type=MESH,
        )

    @pl.when(lower)
    def _():
        for j in range(min(hold_f, ticks)):
            send_pend_f(j).start()

    @pl.when(upper)
    def _():
        for j in range(min(hold_c, ticks)):
            send_pend_c(j).start()

    fcount = ndp * fside * fside
    ccount = ndp * cside * cside

    def save_f(t):
        return pltpu.make_async_copy(fst.at[t], fst_out.at[t], save_sem.at[0, t])

    def save_c(t):
        return pltpu.make_async_copy(cst.at[t], cst_out.at[t], save_sem.at[1, t])

    def first(t, *items):
        @pl.when(t == 0)
        def _():
            for item in items:
                item.wait()

    def front(t):
        first(t, get_fine, get_mixf)

        @pl.when(lower)
        def _():
            @pl.when(jnp.logical_and(seg > 0, t > 0))
            def _():
                send_fo(t - 1).wait_recv()

            xs[...] = fin[t].astype(F32)

        @pl.when(upper)
        def _():
            @pl.when(jnp.logical_and(seg == half, t > 0))
            def _():
                send_up(t - 1).wait_recv()
                spread = dot(upin[t - 1], wu[...])
                width = spread.shape[1] // 4
                for a in range(2):
                    for c in range(2):
                        start = (2 * a + c) * width
                        part = spread[:, start : start + width].reshape(cside, cside, width)
                        for i in range(width // LANES):
                            lanes = slice(i * LANES, (i + 1) * LANES)
                            upscr[i, :, pl.ds(a * fside + c, cside, stride=2), :] = part[:, :, lanes]
                for i in range(width // LANES):
                    lanes = slice(i * LANES, (i + 1) * LANES)
                    fin[t, :, lanes] = upscr[i].reshape(fside * fside, LANES).astype(BF16)

            @pl.when(jnp.logical_and(seg != half, t > 0))
            def _():
                send_fo(t - 1).wait_recv()

            if recv_f:
                first(t, own_pend(9, fine_pend, skf, recv_f))

            @pl.when(t >= recv_f)
            def _():
                send_skf(t - recv_f).wait_recv()

            xs[...] = (dot(fin[t], mixf[...]) + skf[t].astype(F32)).astype(BF16).astype(F32)

        spread_taps(xs[...], colf, fside)
        first(t, get_wf0)
        hf[...] = dot(colf[...], wf[0])
        put_stats(hf[...], statf.at[2 * t])
        exchange(statf.at[2 * t], gotf.at[2 * t], statf_s.at[2 * t], gotf_r.at[2 * t])

    def later(which, t):
        @pl.when(jnp.logical_and(which, t < ticks - 1))
        def _():
            front(t + 1)

    def own_pieces(t):
        @pl.when(t == 0)
        def _():
            get_wf1.wait()

            @pl.when(turn)
            def _():
                get_wd.wait()

            @pl.when(seg == 0)
            def _():
                own_entries.wait()

            @pl.when(seg == half)
            def _():
                get_wu.wait()
                width = wu4.shape[3]
                depth = wuf.shape[1] // 4

                def rows_of(n, carry):
                    rows = pl.multiple_of(n * depth, depth)
                    piece = wu4[pl.ds(rows, depth)].astype(F32).reshape(4 * depth, width)
                    for i in range(width // LANES):
                        wuf[i] = piece[:, i * LANES : (i + 1) * LANES]
                    for q in range(4):
                        for i in range(width // LANES):
                            start = q * width + i * LANES
                            part = wuf[i, pl.ds(q, depth, stride=4), :]
                            wu[pl.ds(rows, depth), start : start + LANES] = part.astype(BF16)
                    return carry

                lax.fori_loop(0, wu4.shape[0] // depth, rows_of, 0)

    front(jnp.int32(0))
    own_pieces(jnp.int32(0))

    def tick(t, carry):
        first(t, get_coarse, get_mixc)

        @pl.when(t > 0)
        def _():
            send_co(t - 1).wait_recv()

        @pl.when(lower)
        def _():
            if recv_c:
                first(t, own_pend(10, coarse_pend, skc, recv_c))

            @pl.when(t >= recv_c)
            def _():
                send_skc(t - recv_c).wait_recv()

            hc[...] = (dot(cin[t], mixc[...]) + skc[t].astype(F32)).astype(BF16).astype(F32)

        @pl.when(upper)
        def _():
            hc[...] = cin[t].astype(F32)

        spread_taps(hc[...], colc, cside)
        first(t, get_wc)
        hc[...] = dot(colc[...], wc[...])
        put_stats(hc[...], statc.at[t])
        exchange(statc.at[t], gotc.at[t], statc_s.at[t], gotc_r.at[t])

        whole(gotf.at[2 * t], statf_s.at[2 * t], gotf_r.at[2 * t]).wait_recv()
        total = statf[2 * t] + jnp.sum(gotf[2 * t], axis=0)
        scale, offset = norm_terms(total, fgain[0:1, :], fshift[0:1, :], fcount)
        xs[...] = jnp.maximum(hf[...] * scale + offset, 0.0).astype(BF16).astype(F32)
        spread_taps(xs[...], colf, fside)
        hg[...] = dot(colf[...], wf[1])
        put_stats(hg[...], statf.at[2 * t + 1])
        exchange(
            statf.at[2 * t + 1], gotf.at[2 * t + 1], statf_s.at[2 * t + 1], gotf_r.at[2 * t + 1]
        )

        whole(gotc.at[t], statc_s.at[t], gotc_r.at[t]).wait_recv()
        total = statc[t] + jnp.sum(gotc[t], axis=0)
        scale, offset = norm_terms(total, cgain[...], cshift[...], ccount)
        cst[t] = jnp.maximum(hc[...] * scale + offset, 0.0).astype(BF16)

        @pl.when(t < ticks - 1)
        def _():
            @pl.when(turn)
            def _():
                send_up(t).start()

            @pl.when(jnp.logical_not(turn))
            def _():
                send_co(t).start()

        save_c(t).start()

        @pl.when(upper)
        def _():
            skc[hold_c + t] = dot(cst[t], mixc[...]).astype(BF16)

            @pl.when(hold_c + t < ticks)
            def _():
                send_skc(hold_c + t).start()

        later(seg == 0, t)

        whole(gotf.at[2 * t + 1], statf_s.at[2 * t + 1], gotf_r.at[2 * t + 1]).wait_recv()
        total = statf[2 * t + 1] + jnp.sum(gotf[2 * t + 1], axis=0)
        scale, offset = norm_terms(total, fgain[1:2, :], fshift[1:2, :], fcount)
        fst[t] = jnp.maximum(hg[...] * scale + offset, 0.0).astype(BF16)

        @pl.when(t < ticks - 1)
        def _():
            @pl.when(turn)
            def _():
                width = fst.shape[2]
                for i in range(width // LANES):
                    lanes = slice(i * LANES, (i + 1) * LANES)
                    upscr[i] = fst[t, :, lanes].astype(F32).reshape(cside, 2 * fside, LANES)
                lowered = None
                for a in range(2):
                    for c in range(2):
                        for i in range(width // LANES):
                            part = upscr[i, :, pl.ds(a * fside + c, cside, stride=2), :]
                            part = part.reshape(cside * cside, LANES).astype(BF16)
                            start = (2 * a + c) * width + i * LANES
                            term = dot(part, wd[start : start + LANES, :])
                            lowered = term if lowered is None else lowered + term
                dbuf[t] = lowered.astype(BF16)
                send_down(t).start()

            @pl.when(jnp.logical_and(jnp.logical_not(turn), seg < nseg - 1))
            def _():
                send_fo(t).start()

        save_f(t).start()

        @pl.when(lower)
        def _():
            skf[hold_f + t] = dot(fst[t], mixf[...]).astype(BF16)

            @pl.when(hold_f + t < ticks)
            def _():
                send_skf(hold_f + t).start()

        later(seg > 0, t)
        return carry

    lax.fori_loop(0, ticks, tick, 0)

    def back_f(first, src):
        return pltpu.make_async_copy(src, fback_out.at[first], save_sem.at[2, first])

    def back_c(first, src):
        return pltpu.make_async_copy(src, cback_out.at[first], save_sem.at[3, first])

    lower_backs = [back_f(j, skf.at[ticks + j]) for j in range(hold_f)]
    lower_backs += [
        back_c(j, skc.at[ticks + j] if j < recv_c else zc) for j in range(hold_c)
    ]
    upper_backs = [
        back_f(j, skf.at[ticks + j] if j < recv_f else zf) for j in range(hold_f)
    ]
    upper_backs += [back_c(j, skc.at[ticks + j]) for j in range(hold_c)]

    @pl.when(lower)
    def _():
        if own_fine:
            own_pend(9, fine_pend, skf, own_fine).wait()
        for j in range(max(ticks - recv_c, 0), ticks):
            send_skc(j).wait_recv()
        for item in lower_backs:
            item.start()
        for j in range(ticks):
            send_skf(j).wait_send()
        for item in lower_backs:
            item.wait()

    @pl.when(upper)
    def _():
        if own_coarse:
            own_pend(10, coarse_pend, skc, own_coarse).wait()
        for j in range(max(ticks - recv_f, 0), ticks):
            send_skf(j).wait_recv()
        for item in upper_backs:
            item.start()
        for j in range(ticks):
            send_skc(j).wait_send()
        for item in upper_backs:
            item.wait()

    @pl.when(turn)
    def _():
        for t in range(ticks - 1):
            send_up(t).wait_send()

    @pl.when(jnp.logical_and(jnp.logical_not(turn), seg < nseg - 1))
    def _():
        for t in range(ticks - 1):
            send_fo(t).wait_send()

    for t in range(ticks - 1):
        send_co(t).wait_send()
    for t in range(ticks):
        whole(gotf.at[2 * t], statf_s.at[2 * t], gotf_r.at[2 * t]).wait_send()
        whole(gotf.at[2 * t + 1], statf_s.at[2 * t + 1], gotf_r.at[2 * t + 1]).wait_send()
        whole(gotc.at[t], statc_s.at[t], gotc_r.at[t]).wait_send()
        save_f(t).wait()
        save_c(t).wait()


def hand_over_kernel(*refs):
    count = (len(refs) - 2) // 3
    sources, results, held = refs[:count], refs[count : 2 * count], refs[2 * count : 3 * count]
    in_sem, out_sem = refs[3 * count :]
    taken, given = [], []
    for i in range(count):
        for j in range(held[i].shape[0]):
            taken.append(pltpu.make_async_copy(sources[i].at[j], held[i].at[j], in_sem.at[i, j]))
            given.append(pltpu.make_async_copy(held[i].at[j], results[i].at[j], out_sem.at[i, j]))
    for item in taken:
        item.start()
    for item, other in zip(taken, given):
        item.wait()
        other.start()
    for item in given:
        item.wait()


def hand_over(arrays):
    most = max(array.shape[0] for array in arrays)
    any_spec = pl.BlockSpec(memory_space=pl.ANY)
    return pl.pallas_call(
        hand_over_kernel,
        out_shape=tuple(jax.ShapeDtypeStruct(a.shape, a.dtype) for a in arrays),
        in_specs=[any_spec] * len(arrays),
        out_specs=(any_spec,) * len(arrays),
        scratch_shapes=[pltpu.VMEM(a.shape, a.dtype) for a in arrays]
        + [pltpu.SemaphoreType.DMA((len(arrays), most))] * 2,
    )(*arrays)


def on_device(
    fine_inflow, coarse_inflow, fine_entries, fine_pending, coarse_pending,
    fine_kernels, fine_mixing, fine_gains, fine_shifts,
    coarse_kernel, coarse_mixing, coarse_gains, coarse_shifts,
    descent_kernel, upsample_kernel,
):
    nseg = lax.axis_size("segment")
    ndp = lax.axis_size("dp")
    half = nseg // 2
    ticks = fine_entries.shape[0] + 1
    hold_f, hold_c = fine_pending.shape[1], coarse_pending.shape[1]
    recv_f, recv_c = 3 * half - hold_f, half - hold_c
    fside, fch = fine_inflow.shape[3], fine_inflow.shape[4]
    cside, cch = coarse_inflow.shape[3], coarse_inflow.shape[4]
    fcells, ccells = fside * fside, cside * cside
    dims = (nseg, ndp, ticks, fside, cside, hold_f, recv_f, hold_c, recv_c)
    frows, crows = 2 * fch // LANES, 2 * cch // LANES
    any_spec = pl.BlockSpec(memory_space=pl.ANY)
    vmem_spec = pl.BlockSpec(memory_space=pltpu.VMEM)
    dma = pltpu.SemaphoreType.DMA
    outs = pl.pallas_call(
        functools.partial(kernel, dims),
        out_shape=(
            jax.ShapeDtypeStruct((ticks, fcells, fch), BF16),
            jax.ShapeDtypeStruct((ticks, ccells, cch), BF16),
            jax.ShapeDtypeStruct((hold_f, fcells, fch), BF16),
            jax.ShapeDtypeStruct((hold_c, ccells, cch), BF16),
        ),
        in_specs=[any_spec] * 7 + [vmem_spec] * 2 + [any_spec] * 2 + [vmem_spec] * 2 + [any_spec] * 2,
        out_specs=(any_spec,) * 4,
        scratch_shapes=[
            pltpu.VMEM((2, 9 * fch, fch), BF16),
            pltpu.VMEM((fch, fch), BF16),
            pltpu.VMEM((9 * cch, cch), BF16),
            pltpu.VMEM((cch, cch), BF16),
            pltpu.VMEM((4 * fch, cch), BF16),
            pltpu.VMEM((cch, 4 * fch), BF16),
            pltpu.VMEM((ticks, fcells, fch), BF16),
            pltpu.VMEM((ticks, ccells, cch), BF16),
            pltpu.VMEM((ticks, ccells, cch), BF16),
            pltpu.VMEM((max(hold_f, recv_f) + ticks, fcells, fch), BF16),
            pltpu.VMEM((max(hold_c, recv_c) + ticks, ccells, cch), BF16),
            pltpu.VMEM((ticks, fcells, fch), BF16),
            pltpu.VMEM((ticks, ccells, cch), BF16),
            pltpu.VMEM((ticks, ccells, cch), BF16),
            pltpu.VMEM((fcells, fch), F32),
            pltpu.VMEM((fcells, fch), F32),
            pltpu.VMEM((fcells, fch), F32),
            pltpu.VMEM((ccells, cch), F32),
            pltpu.VMEM((fch // LANES, cside, 2 * fside, LANES), F32),
            pltpu.VMEM((fcells, 9 * fch), BF16),
            pltpu.VMEM((ccells, 9 * cch), BF16),
            pltpu.VMEM((fcells, fch), BF16),
            pltpu.VMEM((ccells, cch), BF16),
            pltpu.VMEM((2 * ticks, frows, LANES), F32),
            pltpu.VMEM((ticks, crows, LANES), F32),
            pltpu.VMEM((2 * ticks, ndp - 1, frows, LANES), F32),
            pltpu.VMEM((ticks, ndp - 1, crows, LANES), F32),
            pltpu.VMEM((cch, 2, 2, fch), BF16),
            pltpu.VMEM((fch // LANES, 256, LANES), F32),
            dma((12,)),
            dma((4, max(ticks, hold_f, hold_c))),
            dma((ticks,)), dma((ticks,)), dma((ticks,)), dma((ticks,)), dma((ticks,)),
            dma((ticks,)), dma((ticks,)), dma((ticks,)), dma((ticks,)), dma((ticks,)),
            dma((2 * ticks,)), dma((ticks,)), dma((2 * ticks,)), dma((ticks,)),
        ],
        compiler_params=pltpu.CompilerParams(
            collective_id=0, has_side_effects=True, vmem_limit_bytes=56 << 20
        ),
    )(
        fine_inflow.reshape(fcells, fch),
        coarse_inflow.reshape(ccells, cch),
        fine_entries.reshape(ticks - 1, fcells, fch),
        fine_pending.reshape(hold_f, fcells, fch),
        coarse_pending.reshape(hold_c, ccells, cch),
        fine_kernels.reshape(2, 9 * fch, fch),
        fine_mixing.reshape(fch, fch),
        fine_gains.reshape(2, fch),
        fine_shifts.reshape(2, fch),
        coarse_kernel.reshape(9 * cch, cch),
        coarse_mixing.reshape(cch, cch),
        coarse_gains.reshape(1, cch),
        coarse_shifts.reshape(1, cch),
        descent_kernel.reshape(4 * fch, cch),
        upsample_kernel,
    )
    fst, cst, fback, cback = hand_over(outs)
    return (
        fst.reshape(1, ticks, 1, fside, fside, fch),
        cst.reshape(1, ticks, 1, cside, cside, cch),
        fback.reshape(1, hold_f, 1, fside, fside, fch),
        cback.reshape(1, hold_c, 1, cside, cside, cch),
    )


def solution(mesh):
    placed = (
        P("segment", "dp", None, None, None),
        P("segment", "dp", None, None, None),
        P(None, "dp", None, None, None),
        P("segment", None, "dp", None, None, None),
        P("segment", None, "dp", None, None, None),
        P("segment", None, None, None, None, None),
        P("segment", None, None),
        P("segment", None, None),
        P("segment", None, None),
        P("segment", None, None, None, None),
        P("segment", None, None),
        P("segment", None),
        P("segment", None),
        P(),
        P(),
    )
    return jax.shard_map(
        on_device,
        mesh=mesh,
        in_specs=placed,
        out_specs=(
            P("segment", None, "dp", None, None, None),
            P("segment", None, "dp", None, None, None),
            P("segment", None, "dp", None, None, None),
            P("segment", None, "dp", None, None, None),
        ),
        check_vma=False,
    )
```

profile of v0, /device:TPU:2, one launch (start us, length us, event | category | flops | bytes accessed | tf_op | source)
XLA Modules:
  0.0 52.0 jit_solution(164337949478414832)
XLA Ops:
  0.6 49.1 %shard_map.174 = (bf16[4,256,256]{2,1,0:T(8,128)(2,1)}, bf16[4,64,512]{2,1,0:T(8,128)(2,1)}, bf16[2,256,256]{2,1,0:T(8,128)(2,1)}, bf16[1,64,512]{2,1,0:T(8,128)(2,1)}) custom-call(bf16[256,256]{1,0:T(8,128)(2,1)} %bitcast.28, bf16[64,512]{1,0:T(8,128)(2,1)} %bitcast.30, bf16[3,256,256]{2,1,0:T(8,128)(2,1)} %bitcast.26, bf16[2,256,256]{2,1,0:T(8,128)(2,1)} %bitcast.27, ...), custom_call_target="tpu_custom_call" | custom-call | tf_op jit(solution)/shard_map/pallas_call | solution.py:536
  49.8 2.2 %shard_map.175 = (bf16[4,256,256]{2,1,0:T(8,128)(2,1)}, bf16[4,64,512]{2,1,0:T(8,128)(2,1)}, bf16[2,256,256]{2,1,0:T(8,128)(2,1)}, bf16[1,64,512]{2,1,0:T(8,128)(2,1)}) custom-call(bf16[4,256,256]{2,1,0:T(8,128)(2,1)} %get-tuple-element.12.refs_0_, bf16[4,64,512]{2,1,0:T(8,128)(2,1)} %get-tuple-element.13.refs_1_, ...), custom_call_target="tpu_custom_call" | custom-call | tf_op jit(solution)/shard_map/pallas_call | solution.py:506
where the time goes:
time: 52.5 us; the launch traced here: 52 us
  Pallas kernels  51.4 us (98%)
  between operations  0.65 us (1%)
    pallas_call x1, Pallas kernels, on_device(): pl.pallas_call(functools.partial(kernel, dims), out_shape=(jax.ShapeDtype...  49.1 us
    pallas_call x1, Pallas kernels, hand_over(): pl.pallas_call(hand_over_kernel, out_shape=tuple((jax.ShapeDtypeStruct(a....  2.24 us

commit v1 on v0

--- a/solution.py
+++ b/solution.py
@@ -482,6 +482,567 @@
         save_c(t).wait()
 
 
+def sums_of(total):
+    rows = total.shape[0] // 2
+    sums = jnp.concatenate([total[row : row + 1] for row in range(rows)], axis=1)
+    squares = jnp.concatenate([total[rows + row : rows + row + 1] for row in range(rows)], axis=1)
+    return sums, squares
+
+
+def moments(total, count):
+    sums, squares = sums_of(total)
+    center = sums * (1.0 / count)
+    spread = jnp.maximum(squares * (1.0 / count) - center * center, 0.0)
+    return center, lax.rsqrt(spread + EPSILON)
+
+
+def pair_kernel(
+    dims,
+    fine_in, coarse_in, entries, fine_pend, coarse_pend,
+    wf_hbm, mixf_hbm, fgain, fshift, wc_hbm, mixc_hbm, cgain, cshift, wd_hbm, wu_hbm,
+    fst, cst, fback, cback,
+    wf, mixf, wc, mixc, mixm, wd, wu, wu4, wuf,
+    fin, cin, skf, skc, mate_fgain, mate_fshift, mate_cgain, mate_cshift,
+    h1, h2, hc, xs, hx, upscr, colf, colc, cold,
+    rawf_out, rawf_in, rawc_out, rawc_in,
+    st1, st2, stc, got1, got2, gotc, farf, farc,
+    load_sem, s1, r1, s2, r2, sc, rc, sfarf, rfarf, sfarc, rfarc,
+    srawf, rrawf, srawc, rrawc, skf_s, skf_r, one_s, one_r,
+):
+    nseg, ndp, ticks, fside, cside, hold_f, recv_f, hold_c, recv_c = dims
+    seg = lax.axis_index("segment")
+    me = lax.axis_index("dp")
+    other = 1 - seg
+    lower = seg == 0
+    upper = seg == 1
+    fcells, ccells = fside * fside, cside * cside
+    fcount, ccount = ndp * fcells, ndp * ccells
+    last = ticks - 1
+
+    barrier = pltpu.get_barrier_semaphore()
+
+    def greet(k, carry):
+        pl.semaphore_signal(
+            barrier, inc=1, device_id=(seg, lax.rem(me + k, ndp)), device_id_type=MESH
+        )
+        return carry
+
+    def greet_far(k, carry):
+        pl.semaphore_signal(
+            barrier, inc=1, device_id=(other, lax.rem(me + k, ndp)), device_id_type=MESH
+        )
+        return carry
+
+    lax.fori_loop(0, ndp, greet_far, 0)
+    lax.fori_loop(1, ndp, greet, 0)
+
+    def load(k, src, dst):
+        return pltpu.make_async_copy(src, dst, load_sem.at[k])
+
+    get_fine = load(0, fine_in, fin.at[0])
+    get_wf0 = load(1, wf_hbm.at[0], wf.at[0])
+    get_mixf = load(2, mixf_hbm, mixf)
+    get_coarse = load(3, coarse_in, cin)
+    get_mixc = load(4, mixc_hbm, mixc)
+    get_wc = load(5, wc_hbm, wc)
+    get_wf1 = load(6, wf_hbm.at[1], wf.at[1])
+    get_wd = load(7, wd_hbm, wd)
+    get_entries = load(8, entries, fin.at[pl.ds(1, last)])
+    get_pend = load(9, fine_pend.at[pl.ds(0, recv_f)], skf.at[pl.ds(0, recv_f)])
+    get_wu = load(10, wu_hbm, wu4)
+
+    get_fine.start()
+
+    @pl.when(upper)
+    def _():
+        get_mixf.start()
+        get_pend.start()
+
+    get_wf0.start()
+
+    @pl.when(lower)
+    def _():
+        for item in (get_entries, get_wf1, get_mixf, get_coarse, get_mixc, get_wc):
+            item.start()
+
+    @pl.when(upper)
+    def _():
+        for item in (get_coarse, get_wc, get_wf1, get_wd, get_wu, get_mixc):
+            item.start()
+
+    bits = ndp.bit_length() - 1
+
+    def partner(k):
+        if 1 << bits != ndp:
+            return lax.rem(me + k, ndp)
+        to = 0
+        for b in range(bits):
+            step = 1 << b
+            to = to + step * lax.rem(lax.div(me, step) + lax.div(k, step), 2)
+        return to
+
+    def push(src, dst, ssem, rsem):
+        return pltpu.make_async_remote_copy(
+            src_ref=src, dst_ref=dst, send_sem=ssem, recv_sem=rsem,
+            device_id=(other, me), device_id_type=MESH,
+        )
+
+    def share(src, dst, ssem, rsem):
+        def one(i, carry):
+            k = ndp - 1 - i
+            pltpu.make_async_remote_copy(
+                src_ref=src, dst_ref=dst.at[k - 1], send_sem=ssem, recv_sem=rsem,
+                device_id=(seg, partner(k)), device_id_type=MESH,
+            ).start()
+            return carry
+
+        lax.fori_loop(0, ndp - 1, one, 0)
+
+    def cast_far(src, dst, ssem, rsem):
+        def one(i, carry):
+            k = ndp - 1 - i
+            pltpu.make_async_remote_copy(
+                src_ref=src, dst_ref=dst.at[k], send_sem=ssem, recv_sem=rsem,
+                device_id=(other, partner(k)), device_id_type=MESH,
+            ).start()
+            return carry
+
+        lax.fori_loop(0, ndp, one, 0)
+
+    def of_1(t):
+        return push(got1.at[t], got1.at[t], s1.at[t], r1.at[t])
+
+    def of_2(t):
+        return push(got2.at[t], got2.at[t], s2.at[t], r2.at[t])
+
+    def of_c(t):
+        return push(gotc.at[t], gotc.at[t], sc.at[t], rc.at[t])
+
+    def of_farf(t):
+        return push(farf.at[t], farf.at[t], sfarf.at[t], rfarf.at[t])
+
+    def of_farc(t):
+        return push(farc.at[t], farc.at[t], sfarc.at[t], rfarc.at[t])
+
+    def send_rawf(t):
+        return push(rawf_out.at[t], rawf_in.at[t], srawf.at[t], rrawf.at[t])
+
+    def send_rawc(t):
+        return push(rawc_out.at[t], rawc_in.at[t], srawc.at[t], rrawc.at[t])
+
+    def send_skf(j):
+        return push(skf.at[j], skf.at[recv_f + j], skf_s.at[j], skf_r.at[j])
+
+    def send_pend_f(j):
+        return push(fine_pend.at[j], skf.at[recv_f + j], skf_s.at[j], skf_r.at[j])
+
+    send_pend_c = push(coarse_pend.at[0], skc, one_s.at[0], one_r.at[0])
+    send_mix = push(mixc_hbm, mixm, one_s.at[1], one_r.at[1])
+    send_norms = [
+        push(fgain, mate_fgain, one_s.at[2], one_r.at[2]),
+        push(fshift, mate_fshift, one_s.at[3], one_r.at[3]),
+        push(cgain, mate_cgain, one_s.at[4], one_r.at[4]),
+        push(cshift, mate_cshift, one_s.at[5], one_r.at[5]),
+    ]
+
+    def conv_fine(layer, out):
+        spread_taps(xs[...], colf, fside)
+        out[...] = dot(colf[...], wf[layer])
+
+    def conv_coarse(out):
+        spread_taps(hx[...], colc, cside)
+        out[...] = dot(colc[...], wc[...])
+
+    def centred(h, stats, cells):
+        sums, _ = sums_of(stats)
+        return (h - sums * (1.0 / cells)).astype(BF16)
+
+    def arrived(raw, got, gain, shift, count, cells):
+        center, inverse = moments(jnp.sum(got[...], axis=0), count)
+        own, _ = sums_of(got[0])
+        scale = inverse * gain
+        offset = shift + (own * (1.0 / cells) - center) * scale
+        return jnp.maximum(raw[...].astype(F32) * scale + offset, 0.0).astype(BF16)
+
+    def normed(h, stats, got, gain, shift, count):
+        scale, offset = norm_terms(stats[...] + jnp.sum(got[...], axis=0), gain, shift, count)
+        return jnp.maximum(h[...] * scale + offset, 0.0).astype(BF16)
+
+    def first_stats(t):
+        put_stats(h1[t], st1.at[t])
+
+    def first_share(t):
+        share(st1.at[t], got1.at[t], s1.at[t], r1.at[t])
+
+    def second(t):
+        of_1(t).wait_recv()
+        xs[...] = normed(
+            h1.at[t], st1.at[t], got1.at[t], fgain[0:1, :], fshift[0:1, :], fcount
+        ).astype(F32)
+        conv_fine(1, h2.at[t])
+        put_stats(h2[t], st2.at[t])
+
+    def second_share(t):
+        share(st2.at[t], got2.at[t], s2.at[t], r2.at[t])
+
+    def finish_fine(t):
+        of_2(t).wait_recv()
+        fst[t] = normed(h2.at[t], st2.at[t], got2.at[t], fgain[1:2, :], fshift[1:2, :], fcount)
+
+    def finish_coarse(t):
+        of_c(t).wait_recv()
+        cst[t] = normed(hc.at[t], stc.at[t], gotc.at[t], cgain[...], cshift[...], ccount)
+
+    def coarse(t):
+        conv_coarse(hc.at[t])
+        put_stats(hc[t], stc.at[t])
+
+        @pl.when(t < last)
+        def _():
+            cast_far(stc.at[t], farc.at[t], sfarc.at[t], rfarc.at[t])
+            rawc_out[t] = centred(hc[t], stc[t], ccells)
+            send_rawc(t).start()
+
+        share(stc.at[t], gotc.at[t], sc.at[t], rc.at[t])
+
+    def mate_coarse(t):
+        of_farc(t).wait_recv()
+        send_rawc(t).wait_recv()
+        return arrived(rawc_in.at[t], farc.at[t], mate_cgain[...], mate_cshift[...], ccount, ccells)
+
+    get_fine.wait()
+
+    @pl.when(lower)
+    def _():
+        xs[...] = fin[0].astype(F32)
+
+    @pl.when(upper)
+    def _():
+        get_mixf.wait()
+        get_pend.wait()
+        xs[...] = (dot(fin[0], mixf[...]) + skf[0].astype(F32)).astype(BF16).astype(F32)
+
+    get_wf0.wait()
+    conv_fine(0, h1.at[0])
+    first_stats(0)
+    pl.semaphore_wait(barrier, 2 * ndp - 1)
+    first_share(0)
+    for item in send_norms:
+        item.start()
+
+    @pl.when(lower)
+    def _():
+        for j in range(hold_f):
+            send_pend_f(j).start()
+        get_entries.wait()
+
+        def early(t, carry):
+            xs[...] = fin[t].astype(F32)
+            conv_fine(0, h1.at[t])
+            first_stats(t)
+            first_share(t)
+            return carry
+
+        lax.fori_loop(1, ticks, early, 0)
+        for item in (get_wf1, get_mixf, get_coarse, get_mixc, get_wc):
+            item.wait()
+
+        def term(t, carry):
+            finish_fine(t)
+            fresh = dot(fst[t], mixf[...]).astype(BF16)
+
+            @pl.when(hold_f + t < ticks)
+            def _():
+                skf[hold_f + t] = fresh
+                send_skf(hold_f + t).start()
+
+            @pl.when(hold_f + t >= ticks)
+            def _():
+                fback[hold_f + t - ticks] = fresh
+
+            return carry
+
+        def encode(i, carry):
+            @pl.when(i < ticks)
+            def _():
+                second(i)
+
+                @pl.when(i < last)
+                def _():
+                    cast_far(st2.at[i], farf.at[i], sfarf.at[i], rfarf.at[i])
+                    rawf_out[i] = centred(h2[i], st2[i], fcells)
+                    send_rawf(i).start()
+
+                second_share(i)
+
+            t = jnp.maximum(i - last + 1, 0)
+
+            @pl.when(i == 0)
+            def _():
+                send_pend_c.wait_recv()
+                hx[...] = (dot(cin[...], mixc[...]) + skc[...].astype(F32)).astype(BF16).astype(F32)
+
+            @pl.when(i >= last)
+            def _():
+                @pl.when(i == last)
+                def _():
+                    send_mix.wait_recv()
+                    for item in send_norms:
+                        item.wait_recv()
+
+                taken = mate_coarse(t - 1)
+                fresh = dot(taken, mixm[...]).astype(BF16)
+                hx[...] = (dot(taken, mixc[...]) + fresh.astype(F32)).astype(BF16).astype(F32)
+
+            @pl.when(jnp.logical_or(i == 0, i >= last))
+            def _():
+                coarse(t)
+
+            @pl.when(i == last)
+            def _():
+                lax.fori_loop(0, ticks, term, 0)
+                finish_coarse(0)
+
+            @pl.when(i > last)
+            def _():
+                finish_coarse(t - 1)
+
+            return carry
+
+        lax.fori_loop(0, 2 * ticks - 2, encode, 0)
+        cback[...] = jnp.zeros_like(cback)
+        finish_coarse(last)
+        for t in range(last):
+            of_farf(t).wait_send()
+            send_rawf(t).wait_send()
+        for j in range(ticks):
+            send_skf(j).wait_send()
+
+    @pl.when(upper)
+    def _():
+        send_pend_c.start()
+        for item in (get_coarse, get_wc, get_wf1, get_wd, get_wu, get_mixc):
+            item.wait()
+
+        def spread_weights():
+            width = wu4.shape[3]
+            depth = wuf.shape[1] // 4
+
+            def rows_of(n, carry):
+                rows = pl.multiple_of(n * depth, depth)
+                piece = wu4[pl.ds(rows, depth)].astype(F32).reshape(4 * depth, width)
+                for i in range(width // LANES):
+                    wuf[i] = piece[:, i * LANES : (i + 1) * LANES]
+                for q in range(4):
+                    for i in range(width // LANES):
+                        start = q * width + i * LANES
+                        part = wuf[i, pl.ds(q, depth, stride=4), :]
+                        wu[pl.ds(rows, depth), start : start + LANES] = part.astype(BF16)
+                return carry
+
+            lax.fori_loop(0, wu4.shape[0] // depth, rows_of, 0)
+
+        def decode(t, carry):
+            @pl.when(t == 0)
+            def _():
+                hx[...] = cin[...].astype(F32)
+
+            @pl.when(t > 0)
+            def _():
+                @pl.when(t == 1)
+                def _():
+                    for item in send_norms:
+                        item.wait_recv()
+
+                of_farf(t - 1).wait_recv()
+                send_rawf(t - 1).wait_recv()
+                taken = arrived(
+                    rawf_in.at[t - 1], farf.at[t - 1], mate_fgain[1:2, :], mate_fshift[1:2, :],
+                    fcount, fcells,
+                ).astype(F32)
+                width = taken.shape[1]
+                for i in range(width // LANES):
+                    lanes = slice(i * LANES, (i + 1) * LANES)
+                    upscr[i] = taken[:, lanes].reshape(cside, 2 * fside, LANES)
+                for a in range(2):
+                    for c in range(2):
+                        for i in range(width // LANES):
+                            part = upscr[i, :, pl.ds(a * fside + c, cside, stride=2), :]
+                            start = (2 * a + c) * width + i * LANES
+                            cold[:, start : start + LANES] = part.reshape(ccells, LANES).astype(BF16)
+                hx[...] = dot(cold[...], wd[...]).astype(BF16).astype(F32)
+
+            coarse(t)
+
+            @pl.when(t == 0)
+            def _():
+                send_mix.start()
+                spread_weights()
+
+            @pl.when(t == last)
+            def _():
+                finish_fine(0)
+                lax.fori_loop(0, last, lambda n, c: (finish_coarse(n), c)[1], 0)
+
+                def rest(n, c):
+                    finish_fine(n)
+                    return c
+
+                lax.fori_loop(1, last - 1, rest, 0)
+
+            @pl.when(t > 0)
+            def _():
+                @pl.when(t >= recv_f)
+                def _():
+                    send_skf(t - recv_f).wait_recv()
+
+                spread = dot(mate_coarse(t - 1), wu[...])
+                width = spread.shape[1] // 4
+                for a in range(2):
+                    for c in range(2):
+                        start = (2 * a + c) * width
+                        part = spread[:, start : start + width].reshape(cside, cside, width)
+                        for i in range(width // LANES):
+                            lanes = slice(i * LANES, (i + 1) * LANES)
+                            upscr[i, :, pl.ds(a * fside + c, cside, stride=2), :] = part[:, :, lanes]
+                for i in range(width // LANES):
+                    lanes = slice(i * LANES, (i + 1) * LANES)
+                    fin[t, :, lanes] = upscr[i].reshape(fcells, LANES).astype(BF16)
+                xs[...] = (dot(fin[t], mixf[...]) + skf[t].astype(F32)).astype(BF16).astype(F32)
+                conv_fine(0, h1.at[t])
+                first_stats(t)
+                first_share(t)
+
+            n = jnp.where(t < last, t, last) - 1
+
+            @pl.when(t > 0)
+            def _():
+                second(n)
+                second_share(n)
+
+            return carry
+
+        lax.fori_loop(0, ticks, decode, 0)
+        finish_coarse(last)
+        cback[0] = dot(cst[last], mixc[...]).astype(BF16)
+        for j in range(max(ticks - recv_f, 0), ticks):
+            send_skf(j).wait_recv()
+        for j in range(hold_f):
+            fback[j] = skf[ticks + j] if j < recv_f else jnp.zeros_like(skf[0])
+        second(last)
+        second_share(last)
+        finish_fine(last - 1)
+        send_pend_c.wait_send()
+        send_mix.wait_send()
+        finish_fine(last)
+
+    for item in send_norms:
+        item.wait_send()
+    for t in range(ticks):
+        of_1(t).wait_send()
+        of_2(t).wait_send()
+        of_c(t).wait_send()
+    for t in range(last):
+        of_farc(t).wait_send()
+        send_rawc(t).wait_send()
+
+
+def put_out_kernel(*refs):
+    count = (len(refs) - 1) // 2
+    sources, results, sem = refs[:count], refs[count : 2 * count], refs[2 * count]
+    given = [
+        pltpu.make_async_copy(source, result, sem.at[i])
+        for i, (source, result) in enumerate(zip(sources, results))
+    ]
+    for item in given:
+        item.start()
+    for item in given:
+        item.wait()
+
+
+def put_out(arrays):
+    any_spec = pl.BlockSpec(memory_space=pl.ANY)
+    vmem_spec = pl.BlockSpec(memory_space=pltpu.VMEM)
+    held = [pltpu.with_memory_space_constraint(a, pltpu.VMEM) for a in arrays]
+    return pl.pallas_call(
+        put_out_kernel,
+        out_shape=tuple(jax.ShapeDtypeStruct(a.shape, a.dtype) for a in arrays),
+        in_specs=[vmem_spec] * len(arrays),
+        out_specs=(any_spec,) * len(arrays),
+        scratch_shapes=[pltpu.SemaphoreType.DMA((len(arrays),))],
+    )(*held)
+
+
+def run_pair(dims, fch, cch, args):
+    nseg, ndp, ticks, fside, cside, hold_f, recv_f, hold_c, recv_c = dims
+    fcells, ccells = fside * fside, cside * cside
+    frows, crows = 2 * fch // LANES, 2 * cch // LANES
+    last = ticks - 1
+    any_spec = pl.BlockSpec(memory_space=pl.ANY)
+    vmem_spec = pl.BlockSpec(memory_space=pltpu.VMEM)
+    dma, vmem = pltpu.SemaphoreType.DMA, pltpu.VMEM
+    outs = pl.pallas_call(
+        functools.partial(pair_kernel, dims),
+        out_shape=(
+            vmem((ticks, fcells, fch), BF16),
+            vmem((ticks, ccells, cch), BF16),
+            vmem((hold_f, fcells, fch), BF16),
+            vmem((hold_c, ccells, cch), BF16),
+        ),
+        in_specs=[any_spec] * 7 + [vmem_spec] * 2 + [any_spec] * 2 + [vmem_spec] * 2 + [any_spec] * 2,
+        out_specs=(vmem_spec,) * 4,
+        scratch_shapes=[
+            vmem((2, 9 * fch, fch), BF16),
+            vmem((fch, fch), BF16),
+            vmem((9 * cch, cch), BF16),
+            vmem((cch, cch), BF16),
+            vmem((cch, cch), BF16),
+            vmem((4 * fch, cch), BF16),
+            vmem((cch, 4 * fch), BF16),
+            vmem((cch, 2, 2, fch), BF16),
+            vmem((fch // LANES, 256, LANES), F32),
+            vmem((ticks, fcells, fch), BF16),
+            vmem((ccells, cch), BF16),
+            vmem((max(hold_f, recv_f) + ticks, fcells, fch), BF16),
+            vmem((ccells, cch), BF16),
+            vmem((2, fch), F32),
+            vmem((2, fch), F32),
+            vmem((1, cch), F32),
+            vmem((1, cch), F32),
+            vmem((ticks, fcells, fch), F32),
+            vmem((ticks, fcells, fch), F32),
+            vmem((ticks, ccells, cch), F32),
+            vmem((fcells, fch), F32),
+            vmem((ccells, cch), F32),
+            vmem((fch // LANES, cside, 2 * fside, LANES), F32),
+            vmem((fcells, 9 * fch), BF16),
+            vmem((ccells, 9 * cch), BF16),
+            vmem((ccells, 4 * fch), BF16),
+            vmem((last, fcells, fch), BF16),
+            vmem((last, fcells, fch), BF16),
+            vmem((last, ccells, cch), BF16),
+            vmem((last, ccells, cch), BF16),
+            vmem((ticks, frows, LANES), F32),
+            vmem((ticks, frows, LANES), F32),
+            vmem((ticks, crows, LANES), F32),
+            vmem((ticks, ndp - 1, frows, LANES), F32),
+            vmem((ticks, ndp - 1, frows, LANES), F32),
+            vmem((ticks, ndp - 1, crows, LANES), F32),
+            vmem((last, ndp, frows, LANES), F32),
+            vmem((last, ndp, crows, LANES), F32),
+            dma((11,)),
+            dma((ticks,)), dma((ticks,)), dma((ticks,)), dma((ticks,)), dma((ticks,)), dma((ticks,)),
+            dma((last,)), dma((last,)), dma((last,)), dma((last,)),
+            dma((last,)), dma((last,)), dma((last,)), dma((last,)),
+            dma((ticks,)), dma((ticks,)), dma((6,)), dma((6,)),
+        ],
+        compiler_params=pltpu.CompilerParams(
+            collective_id=0, has_side_effects=True, vmem_limit_bytes=56 << 20
+        ),
+    )(*args)
+    return put_out(outs)
+
+
 def hand_over_kernel(*refs):
     count = (len(refs) - 2) // 3
     sources, results, held = refs[:count], refs[count : 2 * count], refs[2 * count : 3 * count]
@@ -533,56 +1094,7 @@
     any_spec = pl.BlockSpec(memory_space=pl.ANY)
     vmem_spec = pl.BlockSpec(memory_space=pltpu.VMEM)
     dma = pltpu.SemaphoreType.DMA
-    outs = pl.pallas_call(
-        functools.partial(kernel, dims),
-        out_shape=(
-            jax.ShapeDtypeStruct((ticks, fcells, fch), BF16),
-            jax.ShapeDtypeStruct((ticks, ccells, cch), BF16),
-            jax.ShapeDtypeStruct((hold_f, fcells, fch), BF16),
-            jax.ShapeDtypeStruct((hold_c, ccells, cch), BF16),
-        ),
-        in_specs=[any_spec] * 7 + [vmem_spec] * 2 + [any_spec] * 2 + [vmem_spec] * 2 + [any_spec] * 2,
-        out_specs=(any_spec,) * 4,
-        scratch_shapes=[
-            pltpu.VMEM((2, 9 * fch, fch), BF16),
-            pltpu.VMEM((fch, fch), BF16),
-            pltpu.VMEM((9 * cch, cch), BF16),
-            pltpu.VMEM((cch, cch), BF16),
-            pltpu.VMEM((4 * fch, cch), BF16),
-            pltpu.VMEM((cch, 4 * fch), BF16),
-            pltpu.VMEM((ticks, fcells, fch), BF16),
-            pltpu.VMEM((ticks, ccells, cch), BF16),
-            pltpu.VMEM((ticks, ccells, cch), BF16),
-            pltpu.VMEM((max(hold_f, recv_f) + ticks, fcells, fch), BF16),
-            pltpu.VMEM((max(hold_c, recv_c) + ticks, ccells, cch), BF16),
-            pltpu.VMEM((ticks, fcells, fch), BF16),
-            pltpu.VMEM((ticks, ccells, cch), BF16),
-            pltpu.VMEM((ticks, ccells, cch), BF16),
-            pltpu.VMEM((fcells, fch), F32),
-            pltpu.VMEM((fcells, fch), F32),
-            pltpu.VMEM((fcells, fch), F32),
-            pltpu.VMEM((ccells, cch), F32),
-            pltpu.VMEM((fch // LANES, cside, 2 * fside, LANES), F32),
-            pltpu.VMEM((fcells, 9 * fch), BF16),
-            pltpu.VMEM((ccells, 9 * cch), BF16),
-            pltpu.VMEM((fcells, fch), BF16),
-            pltpu.VMEM((ccells, cch), BF16),
-            pltpu.VMEM((2 * ticks, frows, LANES), F32),
-            pltpu.VMEM((ticks, crows, LANES), F32),
-            pltpu.VMEM((2 * ticks, ndp - 1, frows, LANES), F32),
-            pltpu.VMEM((ticks, ndp - 1, crows, LANES), F32),
-            pltpu.VMEM((cch, 2, 2, fch), BF16),
-            pltpu.VMEM((fch // LANES, 256, LANES), F32),
-            dma((12,)),
-            dma((4, max(ticks, hold_f, hold_c))),
-            dma((ticks,)), dma((ticks,)), dma((ticks,)), dma((ticks,)), dma((ticks,)),
-            dma((ticks,)), dma((ticks,)), dma((ticks,)), dma((ticks,)), dma((ticks,)),
-            dma((2 * ticks,)), dma((ticks,)), dma((2 * ticks,)), dma((ticks,)),
-        ],
-        compiler_params=pltpu.CompilerParams(
-            collective_id=0, has_side_effects=True, vmem_limit_bytes=56 << 20
-        ),
-    )(
+    args = (
         fine_inflow.reshape(fcells, fch),
         coarse_inflow.reshape(ccells, cch),
         fine_entries.reshape(ticks - 1, fcells, fch),
@@ -599,7 +1111,60 @@
         descent_kernel.reshape(4 * fch, cch),
         upsample_kernel,
     )
-    fst, cst, fback, cback = hand_over(outs)
+    if nseg == 2 and recv_f == 1 and recv_c == 0 and ticks > hold_f + recv_f:
+        fst, cst, fback, cback = run_pair(dims, fch, cch, args)
+    else:
+        outs = pl.pallas_call(
+            functools.partial(kernel, dims),
+            out_shape=(
+                jax.ShapeDtypeStruct((ticks, fcells, fch), BF16),
+                jax.ShapeDtypeStruct((ticks, ccells, cch), BF16),
+                jax.ShapeDtypeStruct((hold_f, fcells, fch), BF16),
+                jax.ShapeDtypeStruct((hold_c, ccells, cch), BF16),
+            ),
+            in_specs=[any_spec] * 7 + [vmem_spec] * 2 + [any_spec] * 2 + [vmem_spec] * 2 + [any_spec] * 2,
+            out_specs=(any_spec,) * 4,
+            scratch_shapes=[
+                pltpu.VMEM((2, 9 * fch, fch), BF16),
+                pltpu.VMEM((fch, fch), BF16),
+                pltpu.VMEM((9 * cch, cch), BF16),
+                pltpu.VMEM((cch, cch), BF16),
+                pltpu.VMEM((4 * fch, cch), BF16),
+                pltpu.VMEM((cch, 4 * fch), BF16),
+                pltpu.VMEM((ticks, fcells, fch), BF16),
+                pltpu.VMEM((ticks, ccells, cch), BF16),
+                pltpu.VMEM((ticks, ccells, cch), BF16),
+                pltpu.VMEM((max(hold_f, recv_f) + ticks, fcells, fch), BF16),
+                pltpu.VMEM((max(hold_c, recv_c) + ticks, ccells, cch), BF16),
+                pltpu.VMEM((ticks, fcells, fch), BF16),
+                pltpu.VMEM((ticks, ccells, cch), BF16),
+                pltpu.VMEM((ticks, ccells, cch), BF16),
+                pltpu.VMEM((fcells, fch), F32),
+                pltpu.VMEM((fcells, fch), F32),
+                pltpu.VMEM((fcells, fch), F32),
+                pltpu.VMEM((ccells, cch), F32),
+                pltpu.VMEM((fch // LANES, cside, 2 * fside, LANES), F32),
+                pltpu.VMEM((fcells, 9 * fch), BF16),
+                pltpu.VMEM((ccells, 9 * cch), BF16),
+                pltpu.VMEM((fcells, fch), BF16),
+                pltpu.VMEM((ccells, cch), BF16),
+                pltpu.VMEM((2 * ticks, frows, LANES), F32),
+                pltpu.VMEM((ticks, crows, LANES), F32),
+                pltpu.VMEM((2 * ticks, ndp - 1, frows, LANES), F32),
+                pltpu.VMEM((ticks, ndp - 1, crows, LANES), F32),
+                pltpu.VMEM((cch, 2, 2, fch), BF16),
+                pltpu.VMEM((fch // LANES, 256, LANES), F32),
+                dma((12,)),
+                dma((4, max(ticks, hold_f, hold_c))),
+                dma((ticks,)), dma((ticks,)), dma((ticks,)), dma((ticks,)), dma((ticks,)),
+                dma((ticks,)), dma((ticks,)), dma((ticks,)), dma((ticks,)), dma((ticks,)),
+                dma((2 * ticks,)), dma((ticks,)), dma((2 * ticks,)), dma((ticks,)),
+            ],
+            compiler_params=pltpu.CompilerParams(
+                collective_id=0, has_side_effects=True, vmem_limit_bytes=56 << 20
+            ),
+        )(*args)
+        fst, cst, fback, cback = hand_over(outs)
     return (
         fst.reshape(1, ticks, 1, fside, fside, fch),
         cst.reshape(1, ticks, 1, cside, cside, cch),

time: 52.5 us -> 50.3 us (0.958)
  Pallas kernels: 51.4 us -> 49.5 us
    pallas_call x2, Pallas kernels: 51.4 us -> 49.5 us  [the longest x1 48.5 us: run_pair(): pl.pallas_call(functools.partial(pair_kernel, dims), out_shape=(vmem((tic...]
where the time goes in v1:
time: 50.3 us; the launch traced here: 50.2 us
  Pallas kernels  49.5 us (98%)
  between operations  0.65 us (1%)
    pallas_call x1, Pallas kernels, run_pair(): pl.pallas_call(functools.partial(pair_kernel, dims), out_shape=(vmem((tic...  48.5 us
    pallas_call x1, Pallas kernels, put_out(): pl.pallas_call(put_out_kernel, out_shape=tuple((jax.ShapeDtypeStruct(a.sh...  1.01 us

profile of v1, /device:TPU:2, one launch (start us, length us, event | category | flops | bytes accessed | tf_op | source)
XLA Modules:
  0.0 50.2 jit_solution(11682155497077312378)
XLA Ops:
  0.6 48.5 %shard_map.174 = (bf16[4,256,256]{2,1,0:T(8,128)(2,1)S(1)}, bf16[4,64,512]{2,1,0:T(8,128)(2,1)S(1)}, bf16[2,256,256]{2,1,0:T(8,128)(2,1)S(1)}, bf16[1,64,512]{2,1,0:T(8,128)(2,1)S(1)}) custom-call(bf16[256,256]{1,0:T(8,128)(2,1)} %bitcast.28, bf16[64,512]{1,0:T(8,128)(2,1)} %bitcast.30, bf16[3,256,256]{2,1,0:T(8,128)(2,1)} %bitcast.26, ...), custom_call_target="tpu_custom_call" | custom-call | tf_op jit(solution)/shard_map/pallas_call | solution.py:984
  49.2 1.0 %shard_map.175 = (bf16[4,256,256]{2,1,0:T(8,128)(2,1)}, bf16[4,64,512]{2,1,0:T(8,128)(2,1)}, bf16[2,256,256]{2,1,0:T(8,128)(2,1)}, bf16[1,64,512]{2,1,0:T(8,128)(2,1)}) custom-call(bf16[4,256,256]{2,1,0:T(8,128)(2,1)S(1)} %get-tuple-element.12.refs_0_, bf16[4,64,512]{2,1,0:T(8,128)(2,1)S(1)} %get-tuple-element.13.refs_1_, ...), custom_call_target="tpu_custom_call" | custom-call | tf_op jit(solution)/shard_map/pallas_call | solution.py:967

commit v2 on v1

--- a/solution.py
+++ b/solution.py
@@ -502,12 +502,12 @@
     wf_hbm, mixf_hbm, fgain, fshift, wc_hbm, mixc_hbm, cgain, cshift, wd_hbm, wu_hbm,
     fst, cst, fback, cback,
     wf, mixf, wc, mixc, mixm, wd, wu, wu4, wuf,
-    fin, cin, skf, skc, mate_fgain, mate_fshift, mate_cgain, mate_cshift,
-    h1, h2, hc, xs, hx, upscr, colf, colc, cold,
+    fin, cin, skf, skc, dbuf, co_in, mate_fgain, mate_fshift, mate_cgain, mate_cshift,
+    hf, hc, xs, hx, upscr, colf, colc, cold,
     rawf_out, rawf_in, rawc_out, rawc_in,
-    st1, st2, stc, got1, got2, gotc, farf, farc,
-    load_sem, s1, r1, s2, r2, sc, rc, sfarf, rfarf, sfarc, rfarc,
-    srawf, rrawf, srawc, rrawc, skf_s, skf_r, one_s, one_r,
+    stf, stc, gotf, gotc, farf, farc,
+    load_sem, sf, rf, sc, rc, sfarf, rfarf, sfarc, rfarc,
+    srawf, rrawf, srawc, rrawc, skf_s, skf_r, dbuf_s, dbuf_r, co_s, co_r, one_s, one_r, ready,
 ):
     nseg, ndp, ticks, fside, cside, hold_f, recv_f, hold_c, recv_c = dims
     seg = lax.axis_index("segment")
@@ -520,21 +520,6 @@
     last = ticks - 1
 
     barrier = pltpu.get_barrier_semaphore()
-
-    def greet(k, carry):
-        pl.semaphore_signal(
-            barrier, inc=1, device_id=(seg, lax.rem(me + k, ndp)), device_id_type=MESH
-        )
-        return carry
-
-    def greet_far(k, carry):
-        pl.semaphore_signal(
-            barrier, inc=1, device_id=(other, lax.rem(me + k, ndp)), device_id_type=MESH
-        )
-        return carry
-
-    lax.fori_loop(0, ndp, greet_far, 0)
-    lax.fori_loop(1, ndp, greet, 0)
 
     def load(k, src, dst):
         return pltpu.make_async_copy(src, dst, load_sem.at[k])
@@ -560,16 +545,6 @@
 
     get_wf0.start()
 
-    @pl.when(lower)
-    def _():
-        for item in (get_entries, get_wf1, get_mixf, get_coarse, get_mixc, get_wc):
-            item.start()
-
-    @pl.when(upper)
-    def _():
-        for item in (get_coarse, get_wc, get_wf1, get_wd, get_wu, get_mixc):
-            item.start()
-
     bits = ndp.bit_length() - 1
 
     def partner(k):
@@ -577,9 +552,25 @@
             return lax.rem(me + k, ndp)
         to = 0
         for b in range(bits):
-            step = 1 << b
-            to = to + step * lax.rem(lax.div(me, step) + lax.div(k, step), 2)
+            bit = lax.rem(lax.div(me, 1 << b), 2)
+            to = to + (1 << b) * (1 - bit if (k >> b) & 1 else bit)
         return to
+
+    partners = [partner(k) for k in range(ndp)]
+    twin = me + 1 - 2 * lax.rem(me, 2)
+    for k in range(ndp - 1, 0, -1):
+        pl.semaphore_signal(barrier, inc=1, device_id=(seg, partners[k]), device_id_type=MESH)
+    pl.semaphore_signal(barrier, inc=1, device_id=(other, me), device_id_type=MESH)
+
+    @pl.when(lower)
+    def _():
+        for item in (get_entries, get_wf1, get_mixf, get_coarse, get_mixc, get_wc, get_wd):
+            item.start()
+
+    @pl.when(upper)
+    def _():
+        for item in (get_coarse, get_wc, get_wf1, get_wd, get_wu, get_mixc):
+            item.start()
 
     def push(src, dst, ssem, rsem):
         return pltpu.make_async_remote_copy(
@@ -588,48 +579,40 @@
         )
 
     def share(src, dst, ssem, rsem):
-        def one(i, carry):
-            k = ndp - 1 - i
+        for k in range(ndp - 1, 0, -1):
             pltpu.make_async_remote_copy(
                 src_ref=src, dst_ref=dst.at[k - 1], send_sem=ssem, recv_sem=rsem,
-                device_id=(seg, partner(k)), device_id_type=MESH,
+                device_id=(seg, partners[k]), device_id_type=MESH,
             ).start()
-            return carry
-
-        lax.fori_loop(0, ndp - 1, one, 0)
 
     def cast_far(src, dst, ssem, rsem):
-        def one(i, carry):
-            k = ndp - 1 - i
+        for k in range(ndp - 1, -1, -1):
             pltpu.make_async_remote_copy(
                 src_ref=src, dst_ref=dst.at[k], send_sem=ssem, recv_sem=rsem,
-                device_id=(other, partner(k)), device_id_type=MESH,
+                device_id=(other, partners[k]), device_id_type=MESH,
             ).start()
-            return carry
-
-        lax.fori_loop(0, ndp, one, 0)
-
-    def of_1(t):
-        return push(got1.at[t], got1.at[t], s1.at[t], r1.at[t])
-
-    def of_2(t):
-        return push(got2.at[t], got2.at[t], s2.at[t], r2.at[t])
+
+    def of_f(n):
+        return push(gotf.at[n], gotf.at[n], sf.at[n], rf.at[n])
 
     def of_c(t):
         return push(gotc.at[t], gotc.at[t], sc.at[t], rc.at[t])
 
-    def of_farf(t):
-        return push(farf.at[t], farf.at[t], sfarf.at[t], rfarf.at[t])
+    of_farf = push(farf, farf, sfarf, rfarf)
+    send_rawf = push(rawf_out, rawf_in, srawf, rrawf)
 
     def of_farc(t):
         return push(farc.at[t], farc.at[t], sfarc.at[t], rfarc.at[t])
 
-    def send_rawf(t):
-        return push(rawf_out.at[t], rawf_in.at[t], srawf.at[t], rrawf.at[t])
+    def send_down(t):
+        return push(dbuf.at[t], dbuf.at[t], dbuf_s.at[t], dbuf_r.at[t])
 
     def send_rawc(t):
         return push(rawc_out.at[t], rawc_in.at[t], srawc.at[t], rrawc.at[t])
 
+    def send_co(t):
+        return push(cst.at[t], co_in.at[t], co_s.at[t], co_r.at[t])
+
     def send_skf(j):
         return push(skf.at[j], skf.at[recv_f + j], skf_s.at[j], skf_r.at[j])
 
@@ -637,7 +620,18 @@
         return push(fine_pend.at[j], skf.at[recv_f + j], skf_s.at[j], skf_r.at[j])
 
     send_pend_c = push(coarse_pend.at[0], skc, one_s.at[0], one_r.at[0])
-    send_mix = push(mixc_hbm, mixm, one_s.at[1], one_r.at[1])
+    part = mixm.shape[0] // 2
+    own_rows = pl.ds(pl.multiple_of(lax.rem(me, 2) * part, part), part)
+    twin_rows = pl.ds(pl.multiple_of(lax.rem(twin, 2) * part, part), part)
+    send_mix = push(mixc_hbm.at[own_rows], mixm.at[own_rows], one_s.at[1], one_r.at[1])
+
+    def hand_mix(rows):
+        return pltpu.make_async_remote_copy(
+            src_ref=mixm.at[rows], dst_ref=mixm.at[rows],
+            send_sem=one_s.at[6], recv_sem=one_r.at[6],
+            device_id=(seg, twin), device_id_type=MESH,
+        )
+
     send_norms = [
         push(fgain, mate_fgain, one_s.at[2], one_r.at[2]),
         push(fshift, mate_fshift, one_s.at[3], one_r.at[3]),
@@ -664,40 +658,50 @@
         offset = shift + (own * (1.0 / cells) - center) * scale
         return jnp.maximum(raw[...].astype(F32) * scale + offset, 0.0).astype(BF16)
 
+    def descended(x):
+        width = x.shape[1]
+        for i in range(width // LANES):
+            lanes = slice(i * LANES, (i + 1) * LANES)
+            upscr[i] = x[:, lanes].reshape(cside, 2 * fside, LANES)
+        for a in range(2):
+            for c in range(2):
+                for i in range(width // LANES):
+                    piece = upscr[i, :, pl.ds(a * fside + c, cside, stride=2), :]
+                    start = (2 * a + c) * width + i * LANES
+                    cold[:, start : start + LANES] = piece.reshape(ccells, LANES).astype(BF16)
+        return dot(cold[...], wd[...]).astype(BF16)
+
     def normed(h, stats, got, gain, shift, count):
         scale, offset = norm_terms(stats[...] + jnp.sum(got[...], axis=0), gain, shift, count)
         return jnp.maximum(h[...] * scale + offset, 0.0).astype(BF16)
 
-    def first_stats(t):
-        put_stats(h1[t], st1.at[t])
-
-    def first_share(t):
-        share(st1.at[t], got1.at[t], s1.at[t], r1.at[t])
-
-    def second(t):
-        of_1(t).wait_recv()
+    def share_fine(n):
+        share(stf.at[n], gotf.at[n], sf.at[n], rf.at[n])
+
+    def conv_stats(layer, n):
+        conv_fine(layer, hf.at[n])
+        put_stats(hf[n], stf.at[n])
+
+    def take_first(t):
+        of_f(t).wait_recv()
         xs[...] = normed(
-            h1.at[t], st1.at[t], got1.at[t], fgain[0:1, :], fshift[0:1, :], fcount
+            hf.at[t], stf.at[t], gotf.at[t], fgain[0:1, :], fshift[0:1, :], fcount
         ).astype(F32)
-        conv_fine(1, h2.at[t])
-        put_stats(h2[t], st2.at[t])
-
-    def second_share(t):
-        share(st2.at[t], got2.at[t], s2.at[t], r2.at[t])
 
     def finish_fine(t):
-        of_2(t).wait_recv()
-        fst[t] = normed(h2.at[t], st2.at[t], got2.at[t], fgain[1:2, :], fshift[1:2, :], fcount)
+        n = ticks + t
+        of_f(n).wait_recv()
+        fst[t] = normed(hf.at[n], stf.at[n], gotf.at[n], fgain[1:2, :], fshift[1:2, :], fcount)
 
     def finish_coarse(t):
         of_c(t).wait_recv()
         cst[t] = normed(hc.at[t], stc.at[t], gotc.at[t], cgain[...], cshift[...], ccount)
 
-    def coarse(t):
+    def coarse(t, raw):
         conv_coarse(hc.at[t])
         put_stats(hc[t], stc.at[t])
 
-        @pl.when(t < last)
+        @pl.when(raw)
         def _():
             cast_far(stc.at[t], farc.at[t], sfarc.at[t], rfarc.at[t])
             rawc_out[t] = centred(hc[t], stc[t], ccells)
@@ -723,38 +727,47 @@
         xs[...] = (dot(fin[0], mixf[...]) + skf[0].astype(F32)).astype(BF16).astype(F32)
 
     get_wf0.wait()
-    conv_fine(0, h1.at[0])
-    first_stats(0)
-    pl.semaphore_wait(barrier, 2 * ndp - 1)
-    first_share(0)
-    for item in send_norms:
-        item.start()
+    conv_stats(0, 0)
+    pl.semaphore_wait(barrier, ndp)
+    share_fine(0)
+    pl.semaphore_signal(ready, inc=1, device_id=(other, me), device_id_type=MESH)
 
     @pl.when(lower)
     def _():
         for j in range(hold_f):
             send_pend_f(j).start()
+        for item in send_norms:
+            item.start()
         get_entries.wait()
 
         def early(t, carry):
             xs[...] = fin[t].astype(F32)
-            conv_fine(0, h1.at[t])
-            first_stats(t)
-            first_share(t)
+            conv_stats(0, t)
+            share_fine(t)
             return carry
 
         lax.fori_loop(1, ticks, early, 0)
-        for item in (get_wf1, get_mixf, get_coarse, get_mixc, get_wc):
+        for item in (get_wf1, get_mixf, get_coarse, get_mixc, get_wc, get_wd):
             item.wait()
+        pl.semaphore_wait(ready, 1)
 
         def term(t, carry):
             finish_fine(t)
+
+            @pl.when(jnp.logical_and(t > 0, t < last))
+            def _():
+                dbuf[t] = descended(fst[t].astype(F32))
+                send_down(t).start()
+
             fresh = dot(fst[t], mixf[...]).astype(BF16)
 
             @pl.when(hold_f + t < ticks)
             def _():
                 skf[hold_f + t] = fresh
-                send_skf(hold_f + t).start()
+
+                @pl.when(t == 0)
+                def _():
+                    send_skf(hold_f).start()
 
             @pl.when(hold_f + t >= ticks)
             def _():
@@ -763,64 +776,92 @@
             return carry
 
         def encode(i, carry):
+            t = jnp.maximum(i - last + 1, 0)
+
             @pl.when(i < ticks)
             def _():
-                second(i)
-
-                @pl.when(i < last)
+                take_first(i)
+                conv_stats(1, ticks + i)
+
+                @pl.when(i == 0)
                 def _():
-                    cast_far(st2.at[i], farf.at[i], sfarf.at[i], rfarf.at[i])
-                    rawf_out[i] = centred(h2[i], st2[i], fcells)
-                    send_rawf(i).start()
-
-                second_share(i)
-
-            t = jnp.maximum(i - last + 1, 0)
+                    cast_far(stf.at[ticks], farf, sfarf, rfarf)
+                    rawf_out[...] = centred(hf[ticks], stf[ticks], fcells)
+                    send_rawf.start()
+
+                share_fine(ticks + i)
+
+            @pl.when(i == last - 1)
+            def _():
+                send_mix.wait_recv()
+                hand_mix(own_rows).start()
 
             @pl.when(i == 0)
             def _():
                 send_pend_c.wait_recv()
                 hx[...] = (dot(cin[...], mixc[...]) + skc[...].astype(F32)).astype(BF16).astype(F32)
 
-            @pl.when(i >= last)
-            def _():
-                @pl.when(i == last)
-                def _():
-                    send_mix.wait_recv()
-                    for item in send_norms:
-                        item.wait_recv()
-
-                taken = mate_coarse(t - 1)
+            def mixed(taken):
                 fresh = dot(taken, mixm[...]).astype(BF16)
                 hx[...] = (dot(taken, mixc[...]) + fresh.astype(F32)).astype(BF16).astype(F32)
 
+            @pl.when(i == last)
+            def _():
+                term(0, 0)
+                hand_mix(twin_rows).wait_recv()
+                for item in send_norms:
+                    item.wait_recv()
+                send_co(0).wait_recv()
+                mixed(co_in[0])
+
+            @pl.when(i > last)
+            def _():
+                finish_coarse(t - 1)
+
+                @pl.when(t < last)
+                def _():
+                    send_co(t - 1).start()
+
+                mixed(mate_coarse(t - 1))
+
             @pl.when(jnp.logical_or(i == 0, i >= last))
             def _():
-                coarse(t)
+                coarse(t, t == last - 1)
 
             @pl.when(i == last)
             def _():
-                lax.fori_loop(0, ticks, term, 0)
                 finish_coarse(0)
-
-            @pl.when(i > last)
-            def _():
-                finish_coarse(t - 1)
+                send_co(0).start()
+                lax.fori_loop(1, ticks, term, 0)
+
+            @pl.when(t == last - 1)
+            def _():
+                for j in range(hold_f + 1, ticks):
+                    send_skf(j).start()
 
             return carry
 
         lax.fori_loop(0, 2 * ticks - 2, encode, 0)
         cback[...] = jnp.zeros_like(cback)
         finish_coarse(last)
-        for t in range(last):
-            of_farf(t).wait_send()
-            send_rawf(t).wait_send()
+        of_farf.wait_send()
+        send_rawf.wait_send()
+        hand_mix(own_rows).wait_send()
+        of_farc(last - 1).wait_send()
+        send_rawc(last - 1).wait_send()
+        for t in range(last - 1):
+            send_co(t).wait_send()
+        for t in range(1, last):
+            send_down(t).wait_send()
         for j in range(ticks):
             send_skf(j).wait_send()
 
     @pl.when(upper)
     def _():
         send_pend_c.start()
+        send_mix.start()
+        for item in send_norms:
+            item.start()
         for item in (get_coarse, get_wc, get_wf1, get_wd, get_wu, get_mixc):
             item.wait()
 
@@ -842,109 +883,136 @@
 
             lax.fori_loop(0, wu4.shape[0] // depth, rows_of, 0)
 
-        def decode(t, carry):
+        pl.semaphore_wait(ready, 1)
+
+        def encode(t, carry):
             @pl.when(t == 0)
             def _():
                 hx[...] = cin[...].astype(F32)
 
-            @pl.when(t > 0)
-            def _():
-                @pl.when(t == 1)
+            @pl.when(t == 1)
+            def _():
+                for item in send_norms:
+                    item.wait_recv()
+                of_farf.wait_recv()
+                send_rawf.wait_recv()
+                taken = arrived(
+                    rawf_in, farf, mate_fgain[1:2, :], mate_fshift[1:2, :], fcount, fcells
+                )
+                hx[...] = descended(taken.astype(F32)).astype(F32)
+
+            @pl.when(t > 1)
+            def _():
+                send_down(t - 1).wait_recv()
+                hx[...] = dbuf[t - 1].astype(F32)
+
+            coarse(t, jnp.logical_and(t > 0, t < last))
+            return carry
+
+        def raised(taken, t):
+            spread = dot(taken, wu[...])
+            width = spread.shape[1] // 4
+            for a in range(2):
+                for c in range(2):
+                    start = (2 * a + c) * width
+                    part = spread[:, start : start + width].reshape(cside, cside, width)
+                    for i in range(width // LANES):
+                        lanes = slice(i * LANES, (i + 1) * LANES)
+                        upscr[i, :, pl.ds(a * fside + c, cside, stride=2), :] = part[:, :, lanes]
+            for i in range(width // LANES):
+                lanes = slice(i * LANES, (i + 1) * LANES)
+                fin[t, :, lanes] = upscr[i].reshape(fcells, LANES).astype(BF16)
+            xs[...] = (dot(fin[t], mixf[...]) + skf[t].astype(F32)).astype(BF16).astype(F32)
+
+        def step(o, carry):
+            coarse_end = jnp.where(o < 2, o + 1, jnp.where(o == 2, ticks, o))
+            lax.fori_loop(o, coarse_end, encode, 0)
+            half_o = lax.div(o, 2)
+            odd = lax.rem(o, 2) == 1
+            is_first = jnp.logical_or(
+                o == 1, jnp.logical_and(jnp.logical_and(o > 1, o < 2 * last), jnp.logical_not(odd))
+            )
+            t = jnp.where(
+                o == 0, 0, jnp.where(is_first, jnp.where(o == 1, 1, half_o + 1),
+                                     jnp.where(o == 2 * last, last, half_o))
+            )
+
+            @pl.when(o == 0)
+            def _():
+                spread_weights()
+
+            @pl.when(o == 1)
+            def _():
+                finish_fine(0)
+
+            @pl.when(o == 2)
+            def _():
+                finish_coarse(1)
+
+            @pl.when(is_first)
+            def _():
+                send_skf(t - recv_f).wait_recv()
+
+                @pl.when(t < last)
                 def _():
-                    for item in send_norms:
-                        item.wait_recv()
-
-                of_farf(t - 1).wait_recv()
-                send_rawf(t - 1).wait_recv()
-                taken = arrived(
-                    rawf_in.at[t - 1], farf.at[t - 1], mate_fgain[1:2, :], mate_fshift[1:2, :],
-                    fcount, fcells,
-                ).astype(F32)
-                width = taken.shape[1]
-                for i in range(width // LANES):
-                    lanes = slice(i * LANES, (i + 1) * LANES)
-                    upscr[i] = taken[:, lanes].reshape(cside, 2 * fside, LANES)
-                for a in range(2):
-                    for c in range(2):
-                        for i in range(width // LANES):
-                            part = upscr[i, :, pl.ds(a * fside + c, cside, stride=2), :]
-                            start = (2 * a + c) * width + i * LANES
-                            cold[:, start : start + LANES] = part.reshape(ccells, LANES).astype(BF16)
-                hx[...] = dot(cold[...], wd[...]).astype(BF16).astype(F32)
-
-            coarse(t)
-
-            @pl.when(t == 0)
-            def _():
-                send_mix.start()
-                spread_weights()
-
-            @pl.when(t == last)
-            def _():
-                finish_fine(0)
-                lax.fori_loop(0, last, lambda n, c: (finish_coarse(n), c)[1], 0)
-
+                    send_co(t - 1).wait_recv()
+                    raised(co_in[t - 1], t)
+
+                @pl.when(t == last)
+                def _():
+                    raised(mate_coarse(t - 1), t)
+
+            @pl.when(jnp.logical_not(is_first))
+            def _():
+                take_first(t)
+
+            layer = jnp.where(is_first, 0, 1)
+            n = layer * ticks + t
+            conv_stats(layer, n)
+            share_fine(n)
+
+            @pl.when(o == 0)
+            def _():
+                finish_coarse(0)
+                send_co(0).start()
+
+            @pl.when(o == 2 * last - 2)
+            def _():
                 def rest(n, c):
+                    finish_coarse(n)
+                    return c
+
+                lax.fori_loop(2, ticks, rest, 0)
+                cback[0] = dot(cst[last], mixc[...]).astype(BF16)
+
+                def rest_fine(n, c):
                     finish_fine(n)
                     return c
 
-                lax.fori_loop(1, last - 1, rest, 0)
-
-            @pl.when(t > 0)
-            def _():
-                @pl.when(t >= recv_f)
-                def _():
-                    send_skf(t - recv_f).wait_recv()
-
-                spread = dot(mate_coarse(t - 1), wu[...])
-                width = spread.shape[1] // 4
-                for a in range(2):
-                    for c in range(2):
-                        start = (2 * a + c) * width
-                        part = spread[:, start : start + width].reshape(cside, cside, width)
-                        for i in range(width // LANES):
-                            lanes = slice(i * LANES, (i + 1) * LANES)
-                            upscr[i, :, pl.ds(a * fside + c, cside, stride=2), :] = part[:, :, lanes]
-                for i in range(width // LANES):
-                    lanes = slice(i * LANES, (i + 1) * LANES)
-                    fin[t, :, lanes] = upscr[i].reshape(fcells, LANES).astype(BF16)
-                xs[...] = (dot(fin[t], mixf[...]) + skf[t].astype(F32)).astype(BF16).astype(F32)
-                conv_fine(0, h1.at[t])
-                first_stats(t)
-                first_share(t)
-
-            n = jnp.where(t < last, t, last) - 1
-
-            @pl.when(t > 0)
-            def _():
-                second(n)
-                second_share(n)
+                lax.fori_loop(1, last - 1, rest_fine, 0)
+                for j in range(max(ticks - recv_f, 0), ticks):
+                    send_skf(j).wait_recv()
+                for j in range(hold_f):
+                    fback[j] = skf[ticks + j] if j < recv_f else jnp.zeros_like(skf[0])
 
             return carry
 
-        lax.fori_loop(0, ticks, decode, 0)
-        finish_coarse(last)
-        cback[0] = dot(cst[last], mixc[...]).astype(BF16)
-        for j in range(max(ticks - recv_f, 0), ticks):
-            send_skf(j).wait_recv()
-        for j in range(hold_f):
-            fback[j] = skf[ticks + j] if j < recv_f else jnp.zeros_like(skf[0])
-        second(last)
-        second_share(last)
+        lax.fori_loop(0, 2 * ticks - 1, step, 0)
         finish_fine(last - 1)
         send_pend_c.wait_send()
         send_mix.wait_send()
+        send_co(0).wait_send()
+        for t in range(1, last):
+            of_farc(t).wait_send()
+            send_rawc(t).wait_send()
         finish_fine(last)
 
     for item in send_norms:
         item.wait_send()
     for t in range(ticks):
-        of_1(t).wait_send()
-        of_2(t).wait_send()
+        of_f(t).wait_send()
+        of_f(ticks + t).wait_send()
         of_c(t).wait_send()
-    for t in range(last):
-        of_farc(t).wait_send()
-        send_rawc(t).wait_send()
 
 
 def put_out_kernel(*refs):
@@ -1005,12 +1073,13 @@
             vmem((ccells, cch), BF16),
             vmem((max(hold_f, recv_f) + ticks, fcells, fch), BF16),
             vmem((ccells, cch), BF16),
+            vmem((ticks, ccells, cch), BF16),
+            vmem((last, ccells, cch), BF16),
             vmem((2, fch), F32),
             vmem((2, fch), F32),
             vmem((1, cch), F32),
             vmem((1, cch), F32),
-            vmem((ticks, fcells, fch), F32),
-            vmem((ticks, fcells, fch), F32),
+            vmem((2 * ticks, fcells, fch), F32),
             vmem((ticks, ccells, cch), F32),
             vmem((fcells, fch), F32),
             vmem((ccells, cch), F32),
@@ -1018,23 +1087,23 @@
             vmem((fcells, 9 * fch), BF16),
             vmem((ccells, 9 * cch), BF16),
             vmem((ccells, 4 * fch), BF16),
-            vmem((last, fcells, fch), BF16),
-            vmem((last, fcells, fch), BF16),
+            vmem((fcells, fch), BF16),
+            vmem((fcells, fch), BF16),
             vmem((last, ccells, cch), BF16),
             vmem((last, ccells, cch), BF16),
-            vmem((ticks, frows, LANES), F32),
-            vmem((ticks, frows, LANES), F32),
+            vmem((2 * ticks, frows, LANES), F32),
             vmem((ticks, crows, LANES), F32),
-            vmem((ticks, ndp - 1, frows, LANES), F32),
-            vmem((ticks, ndp - 1, frows, LANES), F32),
+            vmem((2 * ticks, ndp - 1, frows, LANES), F32),
             vmem((ticks, ndp - 1, crows, LANES), F32),
-            vmem((last, ndp, frows, LANES), F32),
+            vmem((ndp, frows, LANES), F32),
             vmem((last, ndp, crows, LANES), F32),
             dma((11,)),
+            dma((2 * ticks,)), dma((2 * ticks,)), dma((ticks,)), dma((ticks,)),
+            dma, dma, dma((last,)), dma((last,)),
+            dma, dma, dma((last,)), dma((last,)),
             dma((ticks,)), dma((ticks,)), dma((ticks,)), dma((ticks,)), dma((ticks,)), dma((ticks,)),
-            dma((last,)), dma((last,)), dma((last,)), dma((last,)),
-            dma((last,)), dma((last,)), dma((last,)), dma((last,)),
-            dma((ticks,)), dma((ticks,)), dma((6,)), dma((6,)),
+            dma((7,)), dma((7,)),
+            pltpu.SemaphoreType.REGULAR,
         ],
         compiler_params=pltpu.CompilerParams(
             collective_id=0, has_side_effects=True, vmem_limit_bytes=56 << 20
@@ -1111,7 +1180,8 @@
         descent_kernel.reshape(4 * fch, cch),
         upsample_kernel,
     )
-    if nseg == 2 and recv_f == 1 and recv_c == 0 and ticks > hold_f + recv_f:
+    paired = nseg == 2 and ndp % 2 == 0 and recv_f == 1 and recv_c == 0
+    if paired and ticks > hold_f + recv_f:
         fst, cst, fback, cback = run_pair(dims, fch, cch, args)
     else:
         outs = pl.pallas_call(

time: 50.3 us -> 40.7 us (0.81)
  Pallas kernels: 49.5 us -> 39.9 us
    pallas_call x1, Pallas kernels: 48.5 us -> 38.9 us  [run_pair(): pl.pallas_call(functools.partial(pair_kernel, dims), out_shape=(vmem((tic...]
where the time goes in v2:
time: 40.7 us; the launch traced here: 40.6 us
  Pallas kernels  39.9 us (98%)
  between operations  0.65 us (2%)
    pallas_call x1, Pallas kernels, run_pair(): pl.pallas_call(functools.partial(pair_kernel, dims), out_shape=(vmem((tic...  38.9 us
    pallas_call x1, Pallas kernels, put_out(): pl.pallas_call(put_out_kernel, out_shape=tuple((jax.ShapeDtypeStruct(a.sh...  1.01 us

profile of v2, /device:TPU:2, one launch (start us, length us, event | category | flops | bytes accessed | tf_op | source)
XLA Modules:
  0.0 40.6 jit_solution(14050907469598151933)
XLA Ops:
  0.6 38.9 %shard_map.174 = (bf16[4,256,256]{2,1,0:T(8,128)(2,1)S(1)}, bf16[4,64,512]{2,1,0:T(8,128)(2,1)S(1)}, bf16[2,256,256]{2,1,0:T(8,128)(2,1)S(1)}, bf16[1,64,512]{2,1,0:T(8,128)(2,1)S(1)}) custom-call(bf16[256,256]{1,0:T(8,128)(2,1)} %bitcast.28, bf16[64,512]{1,0:T(8,128)(2,1)} %bitcast.30, bf16[3,256,256]{2,1,0:T(8,128)(2,1)} %bitcast.26, ...), custom_call_target="tpu_custom_call" | custom-call | tf_op jit(solution)/shard_map/pallas_call | solution.py:1052
  39.5 1.0 %shard_map.175 = (bf16[4,256,256]{2,1,0:T(8,128)(2,1)}, bf16[4,64,512]{2,1,0:T(8,128)(2,1)}, bf16[2,256,256]{2,1,0:T(8,128)(2,1)}, bf16[1,64,512]{2,1,0:T(8,128)(2,1)}) custom-call(bf16[4,256,256]{2,1,0:T(8,128)(2,1)S(1)} %get-tuple-element.12.refs_0_, bf16[4,64,512]{2,1,0:T(8,128)(2,1)S(1)} %get-tuple-element.13.refs_1_, ...), custom_call_target="tpu_custom_call" | custom-call | tf_op jit(solution)/shard_map/pallas_call | solution.py:1035

commit v3 on v2

--- a/solution.py
+++ b/solution.py
@@ -499,10 +499,11 @@
 def pair_kernel(
     dims,
     fine_in, coarse_in, entries, fine_pend, coarse_pend,
-    wf_hbm, mixf_hbm, fgain, fshift, wc_hbm, mixc_hbm, cgain, cshift, wd_hbm, wu_hbm,
+    wf_hbm, mixf_hbm, fgain_hbm, fshift_hbm, wc_hbm, mixc_hbm, cgain_hbm, cshift_hbm,
+    wd_hbm, wu_hbm,
     fst, cst, fback, cback,
-    wf, mixf, wc, mixc, mixm, wd, wu, wu4, wuf,
-    fin, cin, skf, skc, dbuf, co_in, mate_fgain, mate_fshift, mate_cgain, mate_cshift,
+    wf, mixf, mixe, wc, mixc, mixm, wd, wu, wu4, wuf,
+    fin, cin, skf, skc, dbuf, dbuf_in, co_in, fgain, fshift, cgain, cshift, mate_fgain, mate_fshift, mate_cgain, mate_cshift,
     hf, hc, xs, hx, upscr, colf, colc, cold,
     rawf_out, rawf_in, rawc_out, rawc_in,
     stf, stc, gotf, gotc, farf, farc,
@@ -528,13 +529,17 @@
     get_wf0 = load(1, wf_hbm.at[0], wf.at[0])
     get_mixf = load(2, mixf_hbm, mixf)
     get_coarse = load(3, coarse_in, cin)
-    get_mixc = load(4, mixc_hbm, mixc)
+    get_mixc = load(13, mixc_hbm, mixc)
     get_wc = load(5, wc_hbm, wc)
     get_wf1 = load(6, wf_hbm.at[1], wf.at[1])
     get_wd = load(7, wd_hbm, wd)
     get_entries = load(8, entries, fin.at[pl.ds(1, last)])
-    get_pend = load(9, fine_pend.at[pl.ds(0, recv_f)], skf.at[pl.ds(0, recv_f)])
-    get_wu = load(10, wu_hbm, wu4)
+    get_pend = load(8, fine_pend.at[pl.ds(0, recv_f)], skf.at[pl.ds(0, recv_f)])
+    get_wu = load(9, wu_hbm, wu4)
+    get_norms = [
+        load(10, fgain_hbm, fgain), load(11, fshift_hbm, fshift),
+        load(12, cgain_hbm, cgain), load(4, cshift_hbm, cshift),
+    ]
 
     get_fine.start()
 
@@ -572,6 +577,9 @@
         for item in (get_coarse, get_wc, get_wf1, get_wd, get_wu, get_mixc):
             item.start()
 
+    for item in get_norms:
+        item.start()
+
     def push(src, dst, ssem, rsem):
         return pltpu.make_async_remote_copy(
             src_ref=src, dst_ref=dst, send_sem=ssem, recv_sem=rsem,
@@ -593,67 +601,70 @@
             ).start()
 
     def of_f(n):
-        return push(gotf.at[n], gotf.at[n], sf.at[n], rf.at[n])
+        return push(gotf.at[n], gotf.at[n], sf, rf.at[n])
 
     def of_c(t):
-        return push(gotc.at[t], gotc.at[t], sc.at[t], rc.at[t])
+        return push(gotc.at[t], gotc.at[t], sc, rc.at[t])
 
     of_farf = push(farf, farf, sfarf, rfarf)
     send_rawf = push(rawf_out, rawf_in, srawf, rrawf)
 
     def of_farc(t):
-        return push(farc.at[t], farc.at[t], sfarc.at[t], rfarc.at[t])
+        return push(farc.at[t - 1], farc.at[t - 1], sfarc, rfarc.at[t - 1])
+
+    def send_rawc(t):
+        return push(rawc_out.at[t - 1], rawc_in.at[t - 1], srawc, rrawc.at[t - 1])
 
     def send_down(t):
-        return push(dbuf.at[t], dbuf.at[t], dbuf_s.at[t], dbuf_r.at[t])
-
-    def send_rawc(t):
-        return push(rawc_out.at[t], rawc_in.at[t], srawc.at[t], rrawc.at[t])
+        return push(dbuf.at[t - 1], dbuf_in.at[t - 1], dbuf_s, dbuf_r.at[t - 1])
 
     def send_co(t):
-        return push(cst.at[t], co_in.at[t], co_s.at[t], co_r.at[t])
+        return push(cst.at[t], co_in.at[t], co_s, co_r.at[t])
 
     def send_skf(j):
-        return push(skf.at[j], skf.at[recv_f + j], skf_s.at[j], skf_r.at[j])
+        return push(skf.at[j], skf.at[recv_f + j], skf_s, skf_r.at[j])
 
     def send_pend_f(j):
-        return push(fine_pend.at[j], skf.at[recv_f + j], skf_s.at[j], skf_r.at[j])
+        return push(fine_pend.at[j], skf.at[recv_f + j], skf_s, skf_r.at[j])
 
     send_pend_c = push(coarse_pend.at[0], skc, one_s.at[0], one_r.at[0])
-    part = mixm.shape[0] // 2
-    own_rows = pl.ds(pl.multiple_of(lax.rem(me, 2) * part, part), part)
-    twin_rows = pl.ds(pl.multiple_of(lax.rem(twin, 2) * part, part), part)
-    send_mix = push(mixc_hbm.at[own_rows], mixm.at[own_rows], one_s.at[1], one_r.at[1])
-
-    def hand_mix(rows):
+
+    def rows_of(matrix, device):
+        part = matrix.shape[0] // 2
+        return pl.ds(pl.multiple_of(lax.rem(device, 2) * part, part), part)
+
+    def send_half(src, dst):
+        rows = rows_of(dst, me)
+        return push(src.at[rows], dst.at[rows], one_s.at[1], one_r.at[1])
+
+    def hand_half(matrix, device):
+        rows = rows_of(matrix, device)
         return pltpu.make_async_remote_copy(
-            src_ref=mixm.at[rows], dst_ref=mixm.at[rows],
+            src_ref=matrix.at[rows], dst_ref=matrix.at[rows],
             send_sem=one_s.at[6], recv_sem=one_r.at[6],
             device_id=(seg, twin), device_id_type=MESH,
         )
 
+    send_mixc = send_half(mixc_hbm, mixm)
+    send_mixf = send_half(mixf_hbm, mixe)
     send_norms = [
-        push(fgain, mate_fgain, one_s.at[2], one_r.at[2]),
-        push(fshift, mate_fshift, one_s.at[3], one_r.at[3]),
-        push(cgain, mate_cgain, one_s.at[4], one_r.at[4]),
-        push(cshift, mate_cshift, one_s.at[5], one_r.at[5]),
+        push(fgain_hbm, mate_fgain, one_s.at[2], one_r.at[2]),
+        push(fshift_hbm, mate_fshift, one_s.at[3], one_r.at[3]),
+        push(cgain_hbm, mate_cgain, one_s.at[4], one_r.at[4]),
+        push(cshift_hbm, mate_cshift, one_s.at[5], one_r.at[5]),
     ]
 
     def conv_fine(layer, out):
         spread_taps(xs[...], colf, fside)
         out[...] = dot(colf[...], wf[layer])
 
-    def conv_coarse(out):
-        spread_taps(hx[...], colc, cside)
-        out[...] = dot(colc[...], wc[...])
-
     def centred(h, stats, cells):
         sums, _ = sums_of(stats)
         return (h - sums * (1.0 / cells)).astype(BF16)
 
-    def arrived(raw, got, gain, shift, count, cells):
-        center, inverse = moments(jnp.sum(got[...], axis=0), count)
-        own, _ = sums_of(got[0])
+    def arrived(raw, got, mine, gain, shift, count, cells):
+        center, inverse = moments(got, count)
+        own, _ = sums_of(mine)
         scale = inverse * gain
         offset = shift + (own * (1.0 / cells) - center) * scale
         return jnp.maximum(raw[...].astype(F32) * scale + offset, 0.0).astype(BF16)
@@ -672,18 +683,18 @@
         return dot(cold[...], wd[...]).astype(BF16)
 
     def normed(h, stats, got, gain, shift, count):
-        scale, offset = norm_terms(stats[...] + jnp.sum(got[...], axis=0), gain, shift, count)
-        return jnp.maximum(h[...] * scale + offset, 0.0).astype(BF16)
+        center, inverse = moments(stats[...] + jnp.sum(got[...], axis=0), count)
+        scale = inverse * gain
+        return jnp.maximum(h[...] * scale + (shift - center * scale), 0.0).astype(BF16)
 
     def share_fine(n):
-        share(stf.at[n], gotf.at[n], sf.at[n], rf.at[n])
+        share(stf.at[n], gotf.at[n], sf, rf.at[n])
 
     def conv_stats(layer, n):
         conv_fine(layer, hf.at[n])
         put_stats(hf[n], stf.at[n])
 
     def take_first(t):
-        of_f(t).wait_recv()
         xs[...] = normed(
             hf.at[t], stf.at[t], gotf.at[t], fgain[0:1, :], fshift[0:1, :], fcount
         ).astype(F32)
@@ -698,21 +709,30 @@
         cst[t] = normed(hc.at[t], stc.at[t], gotc.at[t], cgain[...], cshift[...], ccount)
 
     def coarse(t, raw):
-        conv_coarse(hc.at[t])
+        spread_taps(hx[...], colc, cside)
+        hc[t] = dot(colc[...], wc[...])
         put_stats(hc[t], stc.at[t])
 
         @pl.when(raw)
         def _():
-            cast_far(stc.at[t], farc.at[t], sfarc.at[t], rfarc.at[t])
-            rawc_out[t] = centred(hc[t], stc[t], ccells)
+            cast_far(stc.at[t], farc.at[t - 1], sfarc, rfarc.at[t - 1])
+            rawc_out[t - 1] = centred(hc[t], stc[t], ccells)
             send_rawc(t).start()
 
-        share(stc.at[t], gotc.at[t], sc.at[t], rc.at[t])
+        share(stc.at[t], gotc.at[t], sc, rc.at[t])
 
     def mate_coarse(t):
         of_farc(t).wait_recv()
         send_rawc(t).wait_recv()
-        return arrived(rawc_in.at[t], farc.at[t], mate_cgain[...], mate_cshift[...], ccount, ccells)
+        return arrived(
+            rawc_in.at[t - 1], jnp.sum(farc[t - 1], axis=0), farc[t - 1, 0], mate_cgain[...],
+            mate_cshift[...], ccount, ccells,
+        )
+
+    def sent():
+        for item in send_norms:
+            item.wait_send()
+        push(gotc, gotc, sc, rc.at[0]).wait_send()
 
     get_fine.wait()
 
@@ -734,44 +754,48 @@
 
     @pl.when(lower)
     def _():
-        for j in range(hold_f):
-            send_pend_f(j).start()
         for item in send_norms:
             item.start()
+        send_pend_f(0).start()
+        send_mixf.start()
         get_entries.wait()
 
         def early(t, carry):
             xs[...] = fin[t].astype(F32)
             conv_stats(0, t)
-            share_fine(t)
             return carry
 
         lax.fori_loop(1, ticks, early, 0)
-        for item in (get_wf1, get_mixf, get_coarse, get_mixc, get_wc, get_wd):
+        rest = pl.ds(1, last)
+        for k in range(ndp - 1, 0, -1):
+            pltpu.make_async_remote_copy(
+                src_ref=stf.at[rest], dst_ref=gotf.at[rest, k - 1], send_sem=sf, recv_sem=rf.at[1],
+                device_id=(seg, partners[k]), device_id_type=MESH,
+            ).start()
+        for item in (get_wf1, get_mixf, get_coarse, get_mixc, get_wc, get_wd, *get_norms):
             item.wait()
         pl.semaphore_wait(ready, 1)
 
-        def term(t, carry):
+        def term(n, carry):
+            t = jnp.where(n < last - 1, n + 1, jnp.where(n == last, last, 0))
             finish_fine(t)
 
             @pl.when(jnp.logical_and(t > 0, t < last))
             def _():
-                dbuf[t] = descended(fst[t].astype(F32))
+                dbuf[t - 1] = descended(fst[t].astype(F32))
                 send_down(t).start()
 
-            fresh = dot(fst[t], mixf[...]).astype(BF16)
-
-            @pl.when(hold_f + t < ticks)
-            def _():
-                skf[hold_f + t] = fresh
-
-                @pl.when(t == 0)
+            @pl.when(t > 0)
+            def _():
+                fresh = dot(fst[t], mixf[...]).astype(BF16)
+
+                @pl.when(hold_f + t < ticks)
                 def _():
-                    send_skf(hold_f).start()
-
-            @pl.when(hold_f + t >= ticks)
-            def _():
-                fback[hold_f + t - ticks] = fresh
+                    skf[hold_f + t] = fresh
+
+                @pl.when(hold_f + t >= ticks)
+                def _():
+                    fback[hold_f + t - ticks] = fresh
 
             return carry
 
@@ -780,6 +804,14 @@
 
             @pl.when(i < ticks)
             def _():
+                @pl.when(i == 0)
+                def _():
+                    of_f(0).wait_recv()
+
+                @pl.when(i == 1)
+                def _():
+                    push(gotf.at[rest], gotf.at[rest], sf, rf.at[1]).wait_recv()
+
                 take_first(i)
                 conv_stats(1, ticks + i)
 
@@ -791,10 +823,10 @@
 
                 share_fine(ticks + i)
 
-            @pl.when(i == last - 1)
-            def _():
-                send_mix.wait_recv()
-                hand_mix(own_rows).start()
+                @pl.when(i == 1)
+                def _():
+                    for j in range(1, hold_f):
+                        send_pend_f(j).start()
 
             @pl.when(i == 0)
             def _():
@@ -802,13 +834,17 @@
                 hx[...] = (dot(cin[...], mixc[...]) + skc[...].astype(F32)).astype(BF16).astype(F32)
 
             def mixed(taken):
-                fresh = dot(taken, mixm[...]).astype(BF16)
-                hx[...] = (dot(taken, mixc[...]) + fresh.astype(F32)).astype(BF16).astype(F32)
+                hx[...] = dot(taken, mixm[...]).astype(BF16).astype(F32)
 
             @pl.when(i == last)
             def _():
-                term(0, 0)
-                hand_mix(twin_rows).wait_recv()
+                send_mixc.wait_recv()
+                hand_half(mixm, me).start()
+                finish_coarse(0)
+                send_co(0).start()
+                hand_half(mixm, twin).wait_recv()
+                hand_half(mixm, me).wait_send()
+                mixm[...] = (mixm[...].astype(F32) + mixc[...].astype(F32)).astype(BF16)
                 for item in send_norms:
                     item.wait_recv()
                 send_co(0).wait_recv()
@@ -830,11 +866,9 @@
 
             @pl.when(i == last)
             def _():
-                finish_coarse(0)
-                send_co(0).start()
-                lax.fori_loop(1, ticks, term, 0)
-
-            @pl.when(t == last - 1)
+                lax.fori_loop(0, ticks, term, 0)
+
+            @pl.when(t == last)
             def _():
                 for j in range(hold_f + 1, ticks):
                     send_skf(j).start()
@@ -843,27 +877,26 @@
 
         lax.fori_loop(0, 2 * ticks - 2, encode, 0)
         cback[...] = jnp.zeros_like(cback)
-        finish_coarse(last)
         of_farf.wait_send()
         send_rawf.wait_send()
-        hand_mix(own_rows).wait_send()
         of_farc(last - 1).wait_send()
         send_rawc(last - 1).wait_send()
-        for t in range(last - 1):
-            send_co(t).wait_send()
-        for t in range(1, last):
-            send_down(t).wait_send()
-        for j in range(ticks):
-            send_skf(j).wait_send()
+        push(co_in, co_in, co_s, co_r.at[0]).wait_send()
+        push(dbuf, dbuf_in, dbuf_s, dbuf_r.at[0]).wait_send()
+        terms = skf.at[pl.ds(0, ticks - 1)]
+        push(terms, terms, skf_s, skf_r.at[0]).wait_send()
+        send_mixf.wait_send()
+        sent()
+        finish_coarse(last)
 
     @pl.when(upper)
     def _():
-        send_pend_c.start()
-        send_mix.start()
         for item in send_norms:
             item.start()
-        for item in (get_coarse, get_wc, get_wf1, get_wd, get_wu, get_mixc):
-            item.wait()
+        send_pend_c.start()
+        send_mixc.start()
+        get_coarse.wait()
+        get_wc.wait()
 
         def spread_weights():
             width = wu4.shape[3]
@@ -897,14 +930,16 @@
                 of_farf.wait_recv()
                 send_rawf.wait_recv()
                 taken = arrived(
-                    rawf_in, farf, mate_fgain[1:2, :], mate_fshift[1:2, :], fcount, fcells
+                    rawf_in, jnp.sum(farf[...], axis=0), farf[0], mate_fgain[1:2, :],
+                    mate_fshift[1:2, :], fcount, fcells,
                 )
+                fin[0] = taken
                 hx[...] = descended(taken.astype(F32)).astype(F32)
 
             @pl.when(t > 1)
             def _():
                 send_down(t - 1).wait_recv()
-                hx[...] = dbuf[t - 1].astype(F32)
+                hx[...] = dbuf_in[t - 2].astype(F32)
 
             coarse(t, jnp.logical_and(t > 0, t < last))
             return carry
@@ -921,8 +956,8 @@
                         upscr[i, :, pl.ds(a * fside + c, cside, stride=2), :] = part[:, :, lanes]
             for i in range(width // LANES):
                 lanes = slice(i * LANES, (i + 1) * LANES)
-                fin[t, :, lanes] = upscr[i].reshape(fcells, LANES).astype(BF16)
-            xs[...] = (dot(fin[t], mixf[...]) + skf[t].astype(F32)).astype(BF16).astype(F32)
+                part = upscr[i].reshape(fcells, LANES) + skf[t, :, lanes].astype(F32)
+                xs[:, lanes] = part.astype(BF16).astype(F32)
 
         def step(o, carry):
             coarse_end = jnp.where(o < 2, o + 1, jnp.where(o == 2, ticks, o))
@@ -939,11 +974,19 @@
 
             @pl.when(o == 0)
             def _():
+                for item in (get_wf1, get_wd, get_wu, get_mixc, *get_norms):
+                    item.wait()
                 spread_weights()
+                width = mixf.shape[0]
+                for q in range(4):
+                    lanes = slice(q * width, (q + 1) * width)
+                    wu[:, lanes] = dot(wu[:, lanes], mixf[...]).astype(BF16)
 
             @pl.when(o == 1)
             def _():
                 finish_fine(0)
+                hand_half(mixe, twin).wait_recv()
+                skf[recv_f + hold_f] = dot(fin[0], mixe[...]).astype(BF16)
 
             @pl.when(o == 2)
             def _():
@@ -951,7 +994,9 @@
 
             @pl.when(is_first)
             def _():
-                send_skf(t - recv_f).wait_recv()
+                @pl.when(t - recv_f != hold_f)
+                def _():
+                    send_skf(t - recv_f).wait_recv()
 
                 @pl.when(t < last)
                 def _():
@@ -964,6 +1009,7 @@
 
             @pl.when(jnp.logical_not(is_first))
             def _():
+                of_f(t).wait_recv()
                 take_first(t)
 
             layer = jnp.where(is_first, 0, 1)
@@ -975,6 +1021,8 @@
             def _():
                 finish_coarse(0)
                 send_co(0).start()
+                send_mixf.wait_recv()
+                hand_half(mixe, me).start()
 
             @pl.when(o == 2 * last - 2)
             def _():
@@ -985,34 +1033,30 @@
                 lax.fori_loop(2, ticks, rest, 0)
                 cback[0] = dot(cst[last], mixc[...]).astype(BF16)
 
-                def rest_fine(n, c):
-                    finish_fine(n)
-                    return c
-
-                lax.fori_loop(1, last - 1, rest_fine, 0)
-                for j in range(max(ticks - recv_f, 0), ticks):
-                    send_skf(j).wait_recv()
-                for j in range(hold_f):
-                    fback[j] = skf[ticks + j] if j < recv_f else jnp.zeros_like(skf[0])
-
             return carry
 
         lax.fori_loop(0, 2 * ticks - 1, step, 0)
+
+        def rest_fine(n, c):
+            finish_fine(n)
+            return c
+
+        lax.fori_loop(1, last - 1, rest_fine, 0)
+        for j in range(max(ticks - recv_f, 0), ticks):
+            send_skf(j).wait_recv()
+        for j in range(hold_f):
+            fback[j] = skf[ticks + j] if j < recv_f else jnp.zeros_like(skf[0])
         finish_fine(last - 1)
         send_pend_c.wait_send()
-        send_mix.wait_send()
+        send_mixc.wait_send()
+        hand_half(mixe, me).wait_send()
         send_co(0).wait_send()
-        for t in range(1, last):
-            of_farc(t).wait_send()
-            send_rawc(t).wait_send()
+        push(farc, farc, sfarc, rfarc.at[0]).wait_send()
+        push(rawc_in, rawc_in, srawc, rrawc.at[0]).wait_send()
+        sent()
         finish_fine(last)
 
-    for item in send_norms:
-        item.wait_send()
-    for t in range(ticks):
-        of_f(t).wait_send()
-        of_f(ticks + t).wait_send()
-        of_c(t).wait_send()
+    push(gotf, gotf, sf, rf.at[0]).wait_send()
 
 
 def put_out_kernel(*refs):
@@ -1057,10 +1101,11 @@
             vmem((hold_f, fcells, fch), BF16),
             vmem((hold_c, ccells, cch), BF16),
         ),
-        in_specs=[any_spec] * 7 + [vmem_spec] * 2 + [any_spec] * 2 + [vmem_spec] * 2 + [any_spec] * 2,
+        in_specs=[any_spec] * 15,
         out_specs=(vmem_spec,) * 4,
         scratch_shapes=[
             vmem((2, 9 * fch, fch), BF16),
+            vmem((fch, fch), BF16),
             vmem((fch, fch), BF16),
             vmem((9 * cch, cch), BF16),
             vmem((cch, cch), BF16),
@@ -1073,8 +1118,13 @@
             vmem((ccells, cch), BF16),
             vmem((max(hold_f, recv_f) + ticks, fcells, fch), BF16),
             vmem((ccells, cch), BF16),
-            vmem((ticks, ccells, cch), BF16),
-            vmem((last, ccells, cch), BF16),
+            vmem((last - 1, ccells, cch), BF16),
+            vmem((last - 1, ccells, cch), BF16),
+            vmem((last - 1, ccells, cch), BF16),
+            vmem((2, fch), F32),
+            vmem((2, fch), F32),
+            vmem((1, cch), F32),
+            vmem((1, cch), F32),
             vmem((2, fch), F32),
             vmem((2, fch), F32),
             vmem((1, cch), F32),
@@ -1089,19 +1139,19 @@
             vmem((ccells, 4 * fch), BF16),
             vmem((fcells, fch), BF16),
             vmem((fcells, fch), BF16),
-            vmem((last, ccells, cch), BF16),
-            vmem((last, ccells, cch), BF16),
+            vmem((last - 1, ccells, cch), BF16),
+            vmem((last - 1, ccells, cch), BF16),
             vmem((2 * ticks, frows, LANES), F32),
             vmem((ticks, crows, LANES), F32),
             vmem((2 * ticks, ndp - 1, frows, LANES), F32),
             vmem((ticks, ndp - 1, crows, LANES), F32),
             vmem((ndp, frows, LANES), F32),
-            vmem((last, ndp, crows, LANES), F32),
-            dma((11,)),
-            dma((2 * ticks,)), dma((2 * ticks,)), dma((ticks,)), dma((ticks,)),
-            dma, dma, dma((last,)), dma((last,)),
-            dma, dma, dma((last,)), dma((last,)),
-            dma((ticks,)), dma((ticks,)), dma((ticks,)), dma((ticks,)), dma((ticks,)), dma((ticks,)),
+            vmem((last - 1, ndp, crows, LANES), F32),
+            dma((14,)),
+            dma, dma((2 * ticks,)), dma, dma((ticks,)),
+            dma, dma, dma, dma((last - 1,)),
+            dma, dma, dma, dma((last - 1,)),
+            dma, dma((ticks,)), dma, dma((last - 1,)), dma, dma((last - 1,)),
             dma((7,)), dma((7,)),
             pltpu.SemaphoreType.REGULAR,
         ],

time: 40.7 us -> 38.9 us (0.956)
  Pallas kernels: 39.9 us -> 38.1 us
    pallas_call x1, Pallas kernels: 38.9 us -> 37.1 us  [run_pair(): pl.pallas_call(functools.partial(pair_kernel, dims), out_shape=(vmem((tic...]
where the time goes in v3:
time: 38.9 us; the launch traced here: 38.8 us
  Pallas kernels  38.1 us (98%)
  between operations  0.65 us (2%)
    pallas_call x1, Pallas kernels, run_pair(): pl.pallas_call(functools.partial(pair_kernel, dims), out_shape=(vmem((tic...  37.1 us
    pallas_call x1, Pallas kernels, put_out(): pl.pallas_call(put_out_kernel, out_shape=tuple((jax.ShapeDtypeStruct(a.sh...  1.01 us

profile of v3, /device:TPU:2, one launch (start us, length us, event | category | flops | bytes accessed | tf_op | source)
XLA Modules:
  0.0 38.8 jit_solution(11786214502222814138)
XLA Ops:
  0.6 37.1 %shard_map.174 = (bf16[4,256,256]{2,1,0:T(8,128)(2,1)S(1)}, bf16[4,64,512]{2,1,0:T(8,128)(2,1)S(1)}, bf16[2,256,256]{2,1,0:T(8,128)(2,1)S(1)}, bf16[1,64,512]{2,1,0:T(8,128)(2,1)S(1)}) custom-call(bf16[256,256]{1,0:T(8,128)(2,1)} %bitcast.28, bf16[64,512]{1,0:T(8,128)(2,1)} %bitcast.30, bf16[3,256,256]{2,1,0:T(8,128)(2,1)} %bitcast.26, ...), custom_call_target="tpu_custom_call" | custom-call | tf_op jit(solution)/shard_map/pallas_call | solution.py:1096
  37.8 1.0 %shard_map.175 = (bf16[4,256,256]{2,1,0:T(8,128)(2,1)}, bf16[4,64,512]{2,1,0:T(8,128)(2,1)}, bf16[2,256,256]{2,1,0:T(8,128)(2,1)}, bf16[1,64,512]{2,1,0:T(8,128)(2,1)}) custom-call(bf16[4,256,256]{2,1,0:T(8,128)(2,1)S(1)} %get-tuple-element.12.refs_0_, bf16[4,64,512]{2,1,0:T(8,128)(2,1)S(1)} %get-tuple-element.13.refs_1_, ...), custom_call_target="tpu_custom_call" | custom-call | tf_op jit(solution)/shard_map/pallas_call | solution.py:1079

commit v4 on v3

--- a/solution.py
+++ b/solution.py
@@ -503,12 +503,12 @@
     wd_hbm, wu_hbm,
     fst, cst, fback, cback,
     wf, mixf, mixe, wc, mixc, mixm, wd, wu, wu4, wuf,
-    fin, cin, skf, skc, dbuf, dbuf_in, co_in, fgain, fshift, cgain, cshift, mate_fgain, mate_fshift, mate_cgain, mate_cshift,
+    fin, cin, skf, skc, dbuf, dbuf_in, co_in, ec_out, ec_in, fnorm, cnorm, mate_fnorm, mate_cnorm,
     hf, hc, xs, hx, upscr, colf, colc, cold,
     rawf_out, rawf_in, rawc_out, rawc_in,
     stf, stc, gotf, gotc, farf, farc,
-    load_sem, sf, rf, sc, rc, sfarf, rfarf, sfarc, rfarc,
-    srawf, rrawf, srawc, rrawc, skf_s, skf_r, dbuf_s, dbuf_r, co_s, co_r, one_s, one_r, ready,
+    fsum_out, fsum_in,
+    load_sem, rf, rc, rfarf, rfarc, rrawf, rrawc, skf_r, dbuf_r, co_r, one_s, one_r, ready,
 ):
     nseg, ndp, ticks, fside, cside, hold_f, recv_f, hold_c, recv_c = dims
     seg = lax.axis_index("segment")
@@ -519,36 +519,11 @@
     fcells, ccells = fside * fside, cside * cside
     fcount, ccount = ndp * fcells, ndp * ccells
     last = ticks - 1
+    fgain, fshift, cgain, cshift = fnorm.at[0], fnorm.at[1], cnorm.at[0], cnorm.at[1]
+    sf, skf_s, co_s, sc, sfarf = (load_sem.at[k] for k in range(5))
+    sfarc, srawf, srawc, dbuf_s = (load_sem.at[k] for k in range(5, 9))
 
     barrier = pltpu.get_barrier_semaphore()
-
-    def load(k, src, dst):
-        return pltpu.make_async_copy(src, dst, load_sem.at[k])
-
-    get_fine = load(0, fine_in, fin.at[0])
-    get_wf0 = load(1, wf_hbm.at[0], wf.at[0])
-    get_mixf = load(2, mixf_hbm, mixf)
-    get_coarse = load(3, coarse_in, cin)
-    get_mixc = load(13, mixc_hbm, mixc)
-    get_wc = load(5, wc_hbm, wc)
-    get_wf1 = load(6, wf_hbm.at[1], wf.at[1])
-    get_wd = load(7, wd_hbm, wd)
-    get_entries = load(8, entries, fin.at[pl.ds(1, last)])
-    get_pend = load(8, fine_pend.at[pl.ds(0, recv_f)], skf.at[pl.ds(0, recv_f)])
-    get_wu = load(9, wu_hbm, wu4)
-    get_norms = [
-        load(10, fgain_hbm, fgain), load(11, fshift_hbm, fshift),
-        load(12, cgain_hbm, cgain), load(4, cshift_hbm, cshift),
-    ]
-
-    get_fine.start()
-
-    @pl.when(upper)
-    def _():
-        get_mixf.start()
-        get_pend.start()
-
-    get_wf0.start()
 
     bits = ndp.bit_length() - 1
 
@@ -567,6 +542,35 @@
         pl.semaphore_signal(barrier, inc=1, device_id=(seg, partners[k]), device_id_type=MESH)
     pl.semaphore_signal(barrier, inc=1, device_id=(other, me), device_id_type=MESH)
 
+    def load(k, src, dst):
+        return pltpu.make_async_copy(src, dst, load_sem.at[k])
+
+    get_fine = load(0, fine_in, fin.at[0])
+    get_wf0 = load(1, wf_hbm.at[0], wf.at[0])
+    get_mixf = load(2, mixf_hbm, mixf)
+    get_coarse = load(3, coarse_in, cin)
+    get_wc = load(4, wc_hbm, wc)
+    get_wf1 = load(5, wf_hbm.at[1], wf.at[1])
+    get_wd = load(6, wd_hbm, wd)
+    get_entries = load(7, entries, fin.at[pl.ds(1, last)])
+    get_pend = load(7, fine_pend.at[pl.ds(0, recv_f)], skf.at[pl.ds(0, recv_f)])
+    get_norms = [
+        load(8, fgain_hbm, fgain), load(8, fshift_hbm, fshift),
+        load(9, cgain_hbm, cgain), load(9, cshift_hbm, cshift),
+    ]
+    have_norms = [load(8, fnorm, fnorm), load(9, cnorm, cnorm)]
+    get_mixc = load(10, mixc_hbm, mixc)
+    get_wu = load(11, wu_hbm, wu4)
+
+    get_fine.start()
+
+    @pl.when(upper)
+    def _():
+        get_mixf.start()
+        get_pend.start()
+
+    get_wf0.start()
+
     @pl.when(lower)
     def _():
         for item in (get_entries, get_wf1, get_mixf, get_coarse, get_mixc, get_wc, get_wd):
@@ -593,10 +597,10 @@
                 device_id=(seg, partners[k]), device_id_type=MESH,
             ).start()
 
-    def cast_far(src, dst, ssem, rsem):
-        for k in range(ndp - 1, -1, -1):
+    def cast_far(src, dst, ssem, rsem, step=1):
+        for k in range(ndp - step, -1, -step):
             pltpu.make_async_remote_copy(
-                src_ref=src, dst_ref=dst.at[k], send_sem=ssem, recv_sem=rsem,
+                src_ref=src, dst_ref=dst.at[k // step], send_sem=ssem, recv_sem=rsem,
                 device_id=(other, partners[k]), device_id_type=MESH,
             ).start()
 
@@ -641,18 +645,27 @@
         rows = rows_of(matrix, device)
         return pltpu.make_async_remote_copy(
             src_ref=matrix.at[rows], dst_ref=matrix.at[rows],
-            send_sem=one_s.at[6], recv_sem=one_r.at[6],
+            send_sem=one_s.at[4], recv_sem=one_r.at[4],
             device_id=(seg, twin), device_id_type=MESH,
         )
 
-    send_mixc = send_half(mixc_hbm, mixm)
+    def send_mixc(piece):
+        part = mixm.shape[0] // 8
+        start = (4 * lax.rem(me, 2) + 3 * piece) * part
+        rows = pl.ds(pl.multiple_of(start, part), (1 if piece else 3) * part)
+        return push(mixc_hbm.at[rows], mixm.at[rows], one_s.at[1], one_r.at[1])
+
+    all_mixc = send_half(mixc_hbm, mixm)
     send_mixf = send_half(mixf_hbm, mixe)
     send_norms = [
-        push(fgain_hbm, mate_fgain, one_s.at[2], one_r.at[2]),
-        push(fshift_hbm, mate_fshift, one_s.at[3], one_r.at[3]),
-        push(cgain_hbm, mate_cgain, one_s.at[4], one_r.at[4]),
-        push(cshift_hbm, mate_cshift, one_s.at[5], one_r.at[5]),
+        push(fnorm, mate_fnorm, one_s.at[2], one_r.at[2]),
+        push(cnorm, mate_cnorm, one_s.at[3], one_r.at[3]),
     ]
+    send_ec = push(ec_out, ec_in, one_s.at[5], one_r.at[5])
+    share_sum = pltpu.make_async_remote_copy(
+        src_ref=fsum_out, dst_ref=fsum_in, send_sem=one_s.at[6], recv_sem=one_r.at[6],
+        device_id=(seg, twin), device_id_type=MESH,
+    )
 
     def conv_fine(layer, out):
         spread_taps(xs[...], colf, fside)
@@ -725,8 +738,8 @@
         of_farc(t).wait_recv()
         send_rawc(t).wait_recv()
         return arrived(
-            rawc_in.at[t - 1], jnp.sum(farc[t - 1], axis=0), farc[t - 1, 0], mate_cgain[...],
-            mate_cshift[...], ccount, ccells,
+            rawc_in.at[t - 1], jnp.sum(farc[t - 1], axis=0), farc[t - 1, 0], mate_cnorm[0],
+            mate_cnorm[1], ccount, ccells,
         )
 
     def sent():
@@ -754,8 +767,6 @@
 
     @pl.when(lower)
     def _():
-        for item in send_norms:
-            item.start()
         send_pend_f(0).start()
         send_mixf.start()
         get_entries.wait()
@@ -772,8 +783,10 @@
                 src_ref=stf.at[rest], dst_ref=gotf.at[rest, k - 1], send_sem=sf, recv_sem=rf.at[1],
                 device_id=(seg, partners[k]), device_id_type=MESH,
             ).start()
-        for item in (get_wf1, get_mixf, get_coarse, get_mixc, get_wc, get_wd, *get_norms):
+        for item in (get_wf1, get_mixf, get_coarse, get_mixc, get_wc, get_wd, *have_norms):
             item.wait()
+        for item in send_norms:
+            item.start()
         pl.semaphore_wait(ready, 1)
 
         def term(n, carry):
@@ -817,7 +830,7 @@
 
                 @pl.when(i == 0)
                 def _():
-                    cast_far(stf.at[ticks], farf, sfarf, rfarf)
+                    cast_far(stf.at[ticks], farf, sfarf, rfarf, 2)
                     rawf_out[...] = centred(hf[ticks], stf[ticks], fcells)
                     send_rawf.start()
 
@@ -833,32 +846,31 @@
                 send_pend_c.wait_recv()
                 hx[...] = (dot(cin[...], mixc[...]) + skc[...].astype(F32)).astype(BF16).astype(F32)
 
-            def mixed(taken):
-                hx[...] = dot(taken, mixm[...]).astype(BF16).astype(F32)
-
             @pl.when(i == last)
             def _():
-                send_mixc.wait_recv()
-                hand_half(mixm, me).start()
                 finish_coarse(0)
                 send_co(0).start()
-                hand_half(mixm, twin).wait_recv()
-                hand_half(mixm, me).wait_send()
-                mixm[...] = (mixm[...].astype(F32) + mixc[...].astype(F32)).astype(BF16)
                 for item in send_norms:
                     item.wait_recv()
                 send_co(0).wait_recv()
-                mixed(co_in[0])
+                send_ec.wait_recv()
+                hx[...] = (dot(co_in[0], mixc[...]) + ec_in[...].astype(F32)).astype(BF16).astype(F32)
 
             @pl.when(i > last)
             def _():
+                @pl.when(i == last + 1)
+                def _():
+                    hand_half(mixm, twin).wait_recv()
+                    hand_half(mixm, me).wait_send()
+                    mixm[...] = (mixm[...].astype(F32) + mixc[...].astype(F32)).astype(BF16)
+
                 finish_coarse(t - 1)
 
                 @pl.when(t < last)
                 def _():
                     send_co(t - 1).start()
 
-                mixed(mate_coarse(t - 1))
+                hx[...] = dot(mate_coarse(t - 1), mixm[...]).astype(BF16).astype(F32)
 
             @pl.when(jnp.logical_or(i == 0, i >= last))
             def _():
@@ -866,7 +878,10 @@
 
             @pl.when(i == last)
             def _():
-                lax.fori_loop(0, ticks, term, 0)
+                lax.fori_loop(0, ticks - 1, term, 0)
+                all_mixc.wait_recv()
+                hand_half(mixm, me).start()
+                term(last, 0)
 
             @pl.when(t == last)
             def _():
@@ -891,10 +906,8 @@
 
     @pl.when(upper)
     def _():
-        for item in send_norms:
-            item.start()
         send_pend_c.start()
-        send_mixc.start()
+        send_mixc(0).start()
         get_coarse.wait()
         get_wc.wait()
 
@@ -928,10 +941,14 @@
                 for item in send_norms:
                     item.wait_recv()
                 of_farf.wait_recv()
+                fsum_out[...] = jnp.sum(farf[...], axis=0)
+                share_sum.start()
                 send_rawf.wait_recv()
+                share_sum.wait_recv()
+                send_mixc(1).start()
                 taken = arrived(
-                    rawf_in, jnp.sum(farf[...], axis=0), farf[0], mate_fgain[1:2, :],
-                    mate_fshift[1:2, :], fcount, fcells,
+                    rawf_in, fsum_out[...] + fsum_in[...], farf[0], mate_fnorm[0, 1:2, :],
+                    mate_fnorm[1, 1:2, :], fcount, fcells,
                 )
                 fin[0] = taken
                 hx[...] = descended(taken.astype(F32)).astype(F32)
@@ -974,8 +991,10 @@
 
             @pl.when(o == 0)
             def _():
-                for item in (get_wf1, get_wd, get_wu, get_mixc, *get_norms):
+                for item in (get_wf1, get_wd, get_wu, get_mixc, *have_norms):
                     item.wait()
+                for item in send_norms:
+                    item.start()
                 spread_weights()
                 width = mixf.shape[0]
                 for q in range(4):
@@ -1021,6 +1040,8 @@
             def _():
                 finish_coarse(0)
                 send_co(0).start()
+                ec_out[...] = dot(cst[0], mixc[...]).astype(BF16)
+                send_ec.start()
                 send_mixf.wait_recv()
                 hand_half(mixe, me).start()
 
@@ -1048,7 +1069,9 @@
             fback[j] = skf[ticks + j] if j < recv_f else jnp.zeros_like(skf[0])
         finish_fine(last - 1)
         send_pend_c.wait_send()
-        send_mixc.wait_send()
+        all_mixc.wait_send()
+        send_ec.wait_send()
+        share_sum.wait_send()
         hand_half(mixe, me).wait_send()
         send_co(0).wait_send()
         push(farc, farc, sfarc, rfarc.at[0]).wait_send()
@@ -1121,14 +1144,12 @@
             vmem((last - 1, ccells, cch), BF16),
             vmem((last - 1, ccells, cch), BF16),
             vmem((last - 1, ccells, cch), BF16),
-            vmem((2, fch), F32),
-            vmem((2, fch), F32),
-            vmem((1, cch), F32),
-            vmem((1, cch), F32),
-            vmem((2, fch), F32),
-            vmem((2, fch), F32),
-            vmem((1, cch), F32),
-            vmem((1, cch), F32),
+            vmem((ccells, cch), BF16),
+            vmem((ccells, cch), BF16),
+            vmem((2, 2, fch), F32),
+            vmem((2, 1, cch), F32),
+            vmem((2, 2, fch), F32),
+            vmem((2, 1, cch), F32),
             vmem((2 * ticks, fcells, fch), F32),
             vmem((ticks, ccells, cch), F32),
             vmem((fcells, fch), F32),
@@ -1145,14 +1166,12 @@
             vmem((ticks, crows, LANES), F32),
             vmem((2 * ticks, ndp - 1, frows, LANES), F32),
             vmem((ticks, ndp - 1, crows, LANES), F32),
-            vmem((ndp, frows, LANES), F32),
+            vmem((ndp // 2, frows, LANES), F32),
             vmem((last - 1, ndp, crows, LANES), F32),
-            dma((14,)),
-            dma, dma((2 * ticks,)), dma, dma((ticks,)),
-            dma, dma, dma, dma((last - 1,)),
-            dma, dma, dma, dma((last - 1,)),
-            dma, dma((ticks,)), dma, dma((last - 1,)), dma, dma((last - 1,)),
-            dma((7,)), dma((7,)),
+            vmem((frows, LANES), F32),
+            vmem((frows, LANES), F32),
+            dma((12,)), dma((2 * ticks,)), dma((ticks,)), dma, dma((last - 1,)), dma, dma((last - 1,)),
+            dma((ticks,)), dma((last - 1,)), dma((last - 1,)), dma((7,)), dma((7,)),
             pltpu.SemaphoreType.REGULAR,
         ],
         compiler_params=pltpu.CompilerParams(

time: 38.9 us -> 38.4 us (0.987)
  Pallas kernels: 38.1 us -> 37.6 us
    pallas_call x1, Pallas kernels: 37.1 us -> 36.6 us  [run_pair(): pl.pallas_call(functools.partial(pair_kernel, dims), out_shape=(vmem((tic...]
where the time goes in v4:
time: 38.4 us; the launch traced here: 38.2 us
  Pallas kernels  37.6 us (98%)
  between operations  0.65 us (2%)
    pallas_call x1, Pallas kernels, run_pair(): pl.pallas_call(functools.partial(pair_kernel, dims), out_shape=(vmem((tic...  36.6 us
    pallas_call x1, Pallas kernels, put_out(): pl.pallas_call(put_out_kernel, out_shape=tuple((jax.ShapeDtypeStruct(a.sh...  1.01 us

profile of v4, /device:TPU:2, one launch (start us, length us, event | category | flops | bytes accessed | tf_op | source)
XLA Modules:
  0.0 38.2 jit_solution(8840304169285546042)
XLA Ops:
  0.6 36.6 %shard_map.174 = (bf16[4,256,256]{2,1,0:T(8,128)(2,1)S(1)}, bf16[4,64,512]{2,1,0:T(8,128)(2,1)S(1)}, bf16[2,256,256]{2,1,0:T(8,128)(2,1)S(1)}, bf16[1,64,512]{2,1,0:T(8,128)(2,1)S(1)}) custom-call(bf16[256,256]{1,0:T(8,128)(2,1)} %bitcast.28, bf16[64,512]{1,0:T(8,128)(2,1)} %bitcast.30, bf16[3,256,256]{2,1,0:T(8,128)(2,1)} %bitcast.26, ...), custom_call_target="tpu_custom_call" | custom-call | tf_op jit(solution)/shard_map/pallas_call | solution.py:1119
  37.2 1.0 %shard_map.175 = (bf16[4,256,256]{2,1,0:T(8,128)(2,1)}, bf16[4,64,512]{2,1,0:T(8,128)(2,1)}, bf16[2,256,256]{2,1,0:T(8,128)(2,1)}, bf16[1,64,512]{2,1,0:T(8,128)(2,1)}) custom-call(bf16[4,256,256]{2,1,0:T(8,128)(2,1)S(1)} %get-tuple-element.12.refs_0_, bf16[4,64,512]{2,1,0:T(8,128)(2,1)S(1)} %get-tuple-element.13.refs_1_, ...), custom_call_target="tpu_custom_call" | custom-call | tf_op jit(solution)/shard_map/pallas_call | solution.py:1102

commit v5 on v4

--- a/solution.py
+++ b/solution.py
@@ -522,6 +522,7 @@
     fgain, fshift, cgain, cshift = fnorm.at[0], fnorm.at[1], cnorm.at[0], cnorm.at[1]
     sf, skf_s, co_s, sc, sfarf = (load_sem.at[k] for k in range(5))
     sfarc, srawf, srawc, dbuf_s = (load_sem.at[k] for k in range(5, 9))
+    fnorm_s, cnorm_s, hand_s = (load_sem.at[k] for k in range(9, 12))
 
     barrier = pltpu.get_barrier_semaphore()
 
@@ -573,16 +574,15 @@
 
     @pl.when(lower)
     def _():
-        for item in (get_entries, get_wf1, get_mixf, get_coarse, get_mixc, get_wc, get_wd):
+        for item in (
+            get_entries, get_wf1, get_mixf, get_coarse, get_mixc, get_wc, get_wd, *get_norms
+        ):
             item.start()
 
     @pl.when(upper)
     def _():
-        for item in (get_coarse, get_wc, get_wf1, get_wd, get_wu, get_mixc):
-            item.start()
-
-    for item in get_norms:
-        item.start()
+        get_coarse.start()
+        get_wc.start()
 
     def push(src, dst, ssem, rsem):
         return pltpu.make_async_remote_copy(
@@ -631,7 +631,7 @@
     def send_pend_f(j):
         return push(fine_pend.at[j], skf.at[recv_f + j], skf_s, skf_r.at[j])
 
-    send_pend_c = push(coarse_pend.at[0], skc, one_s.at[0], one_r.at[0])
+    send_pend_c = push(coarse_pend.at[0], skc, skf_s, one_r.at[0])
 
     def rows_of(matrix, device):
         part = matrix.shape[0] // 2
@@ -639,13 +639,13 @@
 
     def send_half(src, dst):
         rows = rows_of(dst, me)
-        return push(src.at[rows], dst.at[rows], one_s.at[1], one_r.at[1])
+        return push(src.at[rows], dst.at[rows], one_s, one_r.at[1])
 
     def hand_half(matrix, device):
         rows = rows_of(matrix, device)
         return pltpu.make_async_remote_copy(
             src_ref=matrix.at[rows], dst_ref=matrix.at[rows],
-            send_sem=one_s.at[4], recv_sem=one_r.at[4],
+            send_sem=hand_s, recv_sem=one_r.at[4],
             device_id=(seg, twin), device_id_type=MESH,
         )
 
@@ -653,17 +653,17 @@
         part = mixm.shape[0] // 8
         start = (4 * lax.rem(me, 2) + 3 * piece) * part
         rows = pl.ds(pl.multiple_of(start, part), (1 if piece else 3) * part)
-        return push(mixc_hbm.at[rows], mixm.at[rows], one_s.at[1], one_r.at[1])
+        return push(mixc_hbm.at[rows], mixm.at[rows], one_s, one_r.at[1])
 
     all_mixc = send_half(mixc_hbm, mixm)
     send_mixf = send_half(mixf_hbm, mixe)
     send_norms = [
-        push(fnorm, mate_fnorm, one_s.at[2], one_r.at[2]),
-        push(cnorm, mate_cnorm, one_s.at[3], one_r.at[3]),
+        push(fnorm, mate_fnorm, fnorm_s, one_r.at[2]),
+        push(cnorm, mate_cnorm, cnorm_s, one_r.at[3]),
     ]
-    send_ec = push(ec_out, ec_in, one_s.at[5], one_r.at[5])
+    send_ec = push(ec_out, ec_in, sfarf, one_r.at[5])
     share_sum = pltpu.make_async_remote_copy(
-        src_ref=fsum_out, dst_ref=fsum_in, send_sem=one_s.at[6], recv_sem=one_r.at[6],
+        src_ref=fsum_out, dst_ref=fsum_in, send_sem=srawf, recv_sem=one_r.at[0],
         device_id=(seg, twin), device_id_type=MESH,
     )
 
@@ -910,6 +910,9 @@
         send_mixc(0).start()
         get_coarse.wait()
         get_wc.wait()
+        later = (get_wf1, get_wd, get_wu, get_mixc)
+        for item in (*later, *get_norms):
+            item.start()
 
         def spread_weights():
             width = wu4.shape[3]
@@ -929,8 +932,6 @@
 
             lax.fori_loop(0, wu4.shape[0] // depth, rows_of, 0)
 
-        pl.semaphore_wait(ready, 1)
-
         def encode(t, carry):
             @pl.when(t == 0)
             def _():
@@ -940,6 +941,7 @@
             def _():
                 for item in send_norms:
                     item.wait_recv()
+                pl.semaphore_wait(ready, 1)
                 of_farf.wait_recv()
                 fsum_out[...] = jnp.sum(farf[...], axis=0)
                 share_sum.start()
@@ -991,7 +993,7 @@
 
             @pl.when(o == 0)
             def _():
-                for item in (get_wf1, get_wd, get_wu, get_mixc, *have_norms):
+                for item in (*later, *have_norms):
                     item.wait()
                 for item in send_norms:
                     item.start()
@@ -1171,7 +1173,7 @@
             vmem((frows, LANES), F32),
             vmem((frows, LANES), F32),
             dma((12,)), dma((2 * ticks,)), dma((ticks,)), dma, dma((last - 1,)), dma, dma((last - 1,)),
-            dma((ticks,)), dma((last - 1,)), dma((last - 1,)), dma((7,)), dma((7,)),
+            dma((ticks,)), dma((last - 1,)), dma((last - 1,)), dma, dma((6,)),
             pltpu.SemaphoreType.REGULAR,
         ],
         compiler_params=pltpu.CompilerParams(

time: 38.4 us -> 38.3 us (level)
  no operation moved by 1% of the time
where the time goes in v5:
time: 38.3 us; the launch traced here: 38.2 us
  Pallas kernels  37.5 us (98%)
  between operations  0.65 us (2%)
    pallas_call x1, Pallas kernels, run_pair(): pl.pallas_call(functools.partial(pair_kernel, dims), out_shape=(vmem((tic...  36.5 us
    pallas_call x1, Pallas kernels, put_out(): pl.pallas_call(put_out_kernel, out_shape=tuple((jax.ShapeDtypeStruct(a.sh...  1.01 us

profile of v5, /device:TPU:2, one launch (start us, length us, event | category | flops | bytes accessed | tf_op | source)
XLA Modules:
  0.0 38.2 jit_solution(12295273710226297528)
XLA Ops:
  0.6 36.5 %shard_map.174 = (bf16[4,256,256]{2,1,0:T(8,128)(2,1)S(1)}, bf16[4,64,512]{2,1,0:T(8,128)(2,1)S(1)}, bf16[2,256,256]{2,1,0:T(8,128)(2,1)S(1)}, bf16[1,64,512]{2,1,0:T(8,128)(2,1)S(1)}) custom-call(bf16[256,256]{1,0:T(8,128)(2,1)} %bitcast.28, bf16[64,512]{1,0:T(8,128)(2,1)} %bitcast.30, bf16[3,256,256]{2,1,0:T(8,128)(2,1)} %bitcast.26, ...), custom_call_target="tpu_custom_call" | custom-call | tf_op jit(solution)/shard_map/pallas_call | solution.py:1121
  37.2 1.0 %shard_map.175 = (bf16[4,256,256]{2,1,0:T(8,128)(2,1)}, bf16[4,64,512]{2,1,0:T(8,128)(2,1)}, bf16[2,256,256]{2,1,0:T(8,128)(2,1)}, bf16[1,64,512]{2,1,0:T(8,128)(2,1)}) custom-call(bf16[4,256,256]{2,1,0:T(8,128)(2,1)S(1)} %get-tuple-element.12.refs_0_, bf16[4,64,512]{2,1,0:T(8,128)(2,1)S(1)} %get-tuple-element.13.refs_1_, ...), custom_call_target="tpu_custom_call" | custom-call | tf_op jit(solution)/shard_map/pallas_call | solution.py:1104
